TPU v7x, 256 devices: a whole 4x4x8 slice. The times are simulated.
256 devices in a mesh: tile: 8 (over x, core), dev: 32 (over z, y).
Axes of the slice: x: 4, y: 4, z: 8, core: 2. Of those that a mesh axis runs over, the one named last changes fastest.
Arguments:
- features: bfloat16 [2048, 64, 128], P(('tile', 'dev')), may hold values from -6 to 6
- morton_pos: int32 [2048], P(('tile', 'dev')), may hold values from 0 to 255, as said below
- neighbours: int32 [2048, 27], P(('tile', 'dev')), may hold values from 0 to 24, as said below
- rim: int32 [1024], P(('tile', 'dev')), may hold values from 0 to 7, as said below
- cotangent: bfloat16 [2048, 64, 128], P(('tile', 'dev')), may hold values from -6 to 6
- weight_one: bfloat16 [3456, 128], replicated, may hold values from -0.109375 to 0.109375
- weight_two: bfloat16 [3456, 128], replicated, may hold values from -0.109375 to 0.109375
Outputs:
- output: bfloat16 [2048, 64, 128], P(('tile', 'dev'))
- input_grad: bfloat16 [2048, 64, 128], P(('tile', 'dev'))
- grad_one: float32 [3456, 128], replicated
- grad_two: float32 [3456, 128], replicated
Inputs may be any that keep to these rules, and one draw needn't show every extreme that they name: `morton_pos`: within each super-tile the positions form a permutation of its 256 Morton rows; the 8 scan rows of one device go to at most 2 rows of any one device (position // 8), a bound reached in every draw. `neighbours`: lists come from block coordinates of a sparse map, each device owning a box of 6 x 6 x 2 block cells, tile stepping along x and dev along y: block a's neighbour at offset o is b exactly when b's neighbour at offset 26 - o is a; every block that a neighbouring device reads is in that device's rim list; the four corner columns of every box are empty, so no block reads a device diagonal to its own. `rim`: 4 different blocks of the device.
All inputs are finite; a program needn't handle non-finite values.
Results may differ from a plain program's by a relative error of at most 0.0033.
Values may be sent and summed in bfloat16 or wider, within the bound.
A program may use at most 128 MiB of HBM per device.

v0:
```python
import math

import jax
import jax.numpy as jnp
from jax import lax
from jax.sharding import PartitionSpec as P

EDGE = 4


def with_halo(cells, sides, width):
    for axis, dim in sides:
        count = lax.axis_size(axis)
        ends = count - 1
        head = lax.slice_in_dim(cells, 0, width, axis=dim)
        tail = lax.slice_in_dim(cells, cells.shape[dim] - width, cells.shape[dim], axis=dim)
        cells = jnp.concatenate(
            [
                lax.ppermute(tail, axis, [(i, (i + 1) % count) for i in range(ends)]),
                cells,
                lax.ppermute(head, axis, [((i + 1) % count, i) for i in range(ends)]),
            ],
            axis=dim,
        )
    return cells


def padded_cube(blocks):
    count = blocks.shape[0]
    channels = blocks.shape[-1]
    cube = blocks.reshape(count, 3, 3, 3, EDGE, EDGE, EDGE, channels)
    for axis_pass in range(3):
        cube = jnp.concatenate(
            [cube[:, 0][:, :, :, EDGE - 1 :], cube[:, 1], cube[:, 2][:, :, :, :1]], axis=3
        )
    return cube


def patch_columns(blocks):
    count = blocks.shape[0]
    channels = blocks.shape[-1]
    cube = padded_cube(blocks)
    pieces = [
        cube[:, offset_x : offset_x + EDGE, offset_y : offset_y + EDGE, offset_z : offset_z + EDGE]
        for offset_x in range(3)
        for offset_y in range(3)
        for offset_z in range(3)
    ]
    return jnp.concatenate(pieces, axis=-1).reshape(count * EDGE**3, 27 * channels)


def assemble(own_rows, received):
    empty = jnp.zeros((1,) + own_rows.shape[1:], own_rows.dtype)
    return jnp.concatenate(
        [own_rows, received[0, 1], received[2, 1], received[1, 0], received[1, 2], empty]
    )


def contract_rows(left, right):
    return lax.dot_general(
        left, right, (((0,), (0,)), ((), ())), preferred_element_type=jnp.float32
    )


def per_device(features, morton_pos, neighbours, rim, cotangent, weight_one, weight_two):
    blocks = features.shape[0]
    voxels = features.shape[1]
    channels = features.shape[2]
    rims = rim.shape[0]
    peers = lax.axis_size("dev")
    capacity = 2 * ((blocks + peers - 1) // peers)
    target_dev = morton_pos // blocks
    target_slot = morton_pos % blocks
    onehot = (target_dev[:, None] == jnp.arange(peers, dtype=jnp.int32)[None, :]).astype(jnp.int32)
    earlier = jnp.cumsum(onehot, axis=0) - onehot
    position = jnp.sum(earlier * onehot, axis=1)
    flat_index = target_dev * capacity + position
    outgoing = (
        jnp.zeros((peers * capacity, voxels, channels), jnp.bfloat16).at[flat_index].set(features)
    )
    outgoing = outgoing.reshape(peers, capacity, voxels, channels)
    labels = jnp.full((peers * capacity,), blocks, jnp.int32).at[flat_index].set(target_slot)
    labels = labels.astype(jnp.bfloat16).reshape(peers, capacity)
    arrived, arrived_labels = (
        lax.all_to_all(outgoing, "dev", split_axis=0, concat_axis=0, tiled=True),
        lax.all_to_all(labels, "dev", split_axis=0, concat_axis=0, tiled=True),
    )
    slots = arrived_labels.astype(jnp.int32).reshape(-1)
    morton = jnp.zeros((blocks + 1, voxels, channels), jnp.bfloat16)
    morton = morton.at[slots].set(arrived.reshape(-1, voxels, channels))[:blocks]

    def fetch(own_rows):
        received = with_halo(own_rows[rim][None, None], (("tile", 0), ("dev", 1)), 1)
        return assemble(own_rows, received)

    def columns_of(table):
        return patch_columns(table[neighbours])

    def adjoint(grad_rows, weight):
        flat_grad = grad_rows.reshape(-1, channels)
        back_cols = lax.dot_general(
            flat_grad, weight, (((1,), (1,)), ((), ())), preferred_element_type=jnp.float32
        )
        primal = jnp.zeros((blocks, 27, voxels, channels), jnp.float32)
        unused, pullback = jax.vjp(patch_columns, primal)
        back_blocks = pullback(back_cols)[0]
        total = jnp.zeros((blocks + 4 * rims + 1, voxels, channels), jnp.float32)
        total = total.at[neighbours.reshape(-1)].add(back_blocks.reshape(-1, voxels, channels))
        outward = total[blocks : blocks + 4 * rims].reshape(1, 1, 4, rims, voxels, channels)
        received = with_halo(outward.astype(jnp.bfloat16), (("tile", 0), ("dev", 1)), 1).astype(
            outward.dtype
        )
        returned = received[0, 1, 1] + received[2, 1, 0] + received[1, 0, 3] + received[1, 2, 2]
        own_rows = total[:blocks].at[rim].add(returned)
        return own_rows.reshape(-1, channels)

    cols_input = columns_of(fetch(morton))
    pre_one = jnp.dot(cols_input, weight_one, preferred_element_type=jnp.float32)
    hidden = jax.nn.silu(pre_one).astype(jnp.bfloat16)
    cols_hidden = columns_of(fetch(hidden.reshape(blocks, voxels, channels)))
    pre_two = jnp.dot(cols_hidden, weight_two, preferred_element_type=jnp.float32)
    output = (morton.reshape(-1, channels).astype(jnp.float32) + pre_two).astype(jnp.bfloat16)
    output = output.reshape(blocks, voxels, channels)
    grad_flat = cotangent.reshape(-1, channels)
    grad_two = contract_rows(cols_hidden, grad_flat)
    hidden_grad = adjoint(cotangent, weight_two)
    gate = jax.nn.sigmoid(pre_one)
    pre_grad = (hidden_grad * gate * (1.0 + pre_one * (1.0 - gate))).astype(jnp.bfloat16)
    grad_one = contract_rows(cols_input, pre_grad)
    morton_part = adjoint(pre_grad.reshape(blocks, voxels, channels), weight_one)
    morton_grad = (morton_part + grad_flat.astype(jnp.float32)).astype(jnp.bfloat16)
    morton_grad = morton_grad.reshape(blocks, voxels, channels)
    padded_rows = jnp.concatenate([morton_grad, jnp.zeros((1, voxels, channels), jnp.bfloat16)])
    returning = padded_rows[slots].reshape(peers, capacity, voxels, channels)
    coming_back = lax.all_to_all(returning, "dev", split_axis=0, concat_axis=0, tiled=True)
    input_grad = coming_back.reshape(-1, voxels, channels)[flat_index]
    summed = lax.psum((grad_one, grad_two), ("tile", "dev"))
    scale = 1.0 / math.sqrt(blocks * voxels * lax.axis_size("tile") * peers)
    return (output, input_grad, summed[0] * scale, summed[1] * scale)


def solution(mesh):
    placed = (
        P(("tile", "dev"), None, None),
        P(("tile", "dev")),
        P(("tile", "dev"), None),
        P(("tile", "dev")),
        P(("tile", "dev"), None, None),
        P(),
        P(),
    )
    return jax.shard_map(
        per_device,
        mesh=mesh,
        in_specs=placed,
        out_specs=(P(("tile", "dev"), None, None), P(("tile", "dev"), None, None), P(), P()),
        check_vma=False,
    )
```

profile of v0, /device:TPU:2, one launch (start us, length us, event | category | flops | bytes accessed | tf_op | source)
XLA Modules:
  0.0 551.4 jit_solution(1049707976874400269)
XLA Ops:
  9.6 11.5 %all-to-all-start = ((bf16[32,1,2]{2,1,0:T(2,128)(2,1)}), bf16[32,1,2]{2,1,0:T(2,128)(2,1)S(1)}, u32[]{:S(2)}, u32[]{:S(2)}) async-start(bf16[32,1,2]{2,1,0:T(2,128)(2,1)} %all_to_all.16), calls=%async_computation | async-start | bytes 32768 | tf_op jit(solution)/shard_map/all_to_all | solution.py:86
  32.5 9.9 %all-to-all-start.1 = ((bf16[32,2,64,128]{3,2,1,0:T(8,128)(2,1)}), bf16[32,2,64,128]{3,2,1,0:T(8,128)(2,1)}, u32[]{:S(2)}, u32[]{:S(2)}) async-start(bf16[32,2,64,128]{3,2,1,0:T(8,128)(2,1)} %bitcast.161), calls=%async_computation.1 | async-start | bytes 2097152 | tf_op jit(solution)/shard_map/all_to_all | solution.py:85
  49.0 4.8 copy.46
  53.8 23.3 %scatter_fusion.2 = f32[25,64,128]{2,1,0:T(8,128)S(1)} fusion(f32[25,64,128]{2,1,0:T(8,128)S(1)} %broadcast.271.clone, s32[216]{0:T(256)S(1)} %bitcast.179, f32[216,64,128]{2,1,0:T(8,128)} %bitcast.157), kind=kCustom, calls=%fused_computation.9 | custom fusion | flops 1769472 | bytes 21234528 | tf_op jit(solution)/shard_map/scatter-add | solution.py:108
  83.0 3.8 collective-permute-done.8
  89.1 5.4 collective-permute-start.10
  95.4 6.3 %scatter_fusion.1 = bf16[9,64,128]{2,1,0:T(8,128)(2,1)S(1)} fusion(bf16[9,64,128]{2,1,0:T(8,128)(2,1)S(1)} %broadcast_in_dim.90, s32[64]{0:T(128)S(1)} %fusion.43, bf16[64,64,128]{2,1,0:T(8,128)(2,1)} %bitcast.2), kind=kCustom, calls=%fused_computation.8 | custom fusion | bytes 3145984 | tf_op jit(solution)/shard_map/scatter | solution.py:90
  113.7 5.2 collective-permute-start.2
  118.9 2.9 collective-permute-done.2
  122.0 2.8 gather_fusion.1
  124.8 4.4 slice_bitcast_fusion.9
  154.4 6.6 %reshape.159 = bf16[512,3456]{1,0:T(8,128)(2,1)} reshape(bf16[8,4,4,4,3456]{4,3,2,1,0:T(4,128)(2,1)} %constant_dynamic-update-slice_fusion.6) | data formatting | bytes 7077888 | tf_op jit(solution)/shard_map/reshape | solution.py:49
  161.0 3.1 fusion.4
  169.3 4.3 fusion.54
  173.6 4.0 fusion.53
  177.6 8.7 %reshape.167 = f32[8,4,4,4,3456]{4,3,2,1,0:T(4,128)} reshape(f32[512,3456]{1,0:T(8,128)} %fusion.53) | data formatting | bytes 14155776 | tf_op jit(solution)/shard_map/transpose(jvp())/reshape | solution.py:49
  188.3 3.6 fusion.46
  202.3 5.0 collective-permute-start.6
  207.3 5.1 collective-permute-done.6
  215.3 4.4 slice_bitcast_fusion.6
  245.2 6.7 %reshape.162 = bf16[512,3456]{1,0:T(8,128)(2,1)} reshape(bf16[8,4,4,4,3456]{4,3,2,1,0:T(4,128)(2,1)} %constant_dynamic-update-slice_fusion.39) | data formatting | bytes 7077888 | tf_op jit(solution)/shard_map/reshape | solution.py:49
  251.9 4.3 fusion.55
  256.3 4.4 pad_add_fusion
  260.7 4.4 copy.47
  265.2 23.6 %scatter_fusion.4 = f32[25,64,128]{2,1,0:T(8,128)S(1)} fusion(f32[25,64,128]{2,1,0:T(8,128)S(1)} %broadcast.271, s32[216]{0:T(256)S(1)} %bitcast.180, f32[216,64,128]{2,1,0:T(8,128)} %bitcast.158), kind=kCustom, calls=%fused_computation.11 | custom fusion | flops 1769472 | bytes 21234528 | tf_op jit(solution)/shard_map/scatter-add | solution.py:108
  294.8 4.0 collective-permute-done.12
  300.2 4.8 collective-permute-start.14
  305.1 16.5 %collective-permute-done.15 = bf16[3,1,4,4,64,128]{5,4,3,2,1,0:T(8,128)(2,1)S(1)} collective-permute-done((bf16[3,1,4,4,64,128]{5,4,3,2,1,0:T(8,128)(2,1)S(1)}, bf16[3,1,4,4,64,128]{5,4,3,2,1,0:T(8,128)(2,1)S(1)}, u32[]{:S(2)}, u32[]{:S(2)}) %collective-permute-start.15) | collective-permute-done | bytes 786464 | tf_op jit(solution)/shard_map/ppermute | solution.py:21
  324.7 24.2 %all-to-all-start.2 = ((bf16[32,2,64,128]{3,2,1,0:T(8,128)(2,1)}), bf16[32,2,64,128]{3,2,1,0:T(8,128)(2,1)S(1)}, u32[]{:S(2)}, u32[]{:S(2)}) async-start(bf16[32,2,64,128]{3,2,1,0:T(8,128)(2,1)} %bitcast.65), calls=%async_computation.2 | async-start | bytes 2097152 | tf_op jit(solution)/shard_map/all_to_all | solution.py:135
  348.9 3.8 fusion
  352.7 186.1 %all-reduce.88.cloned.1.call-done = (f32[3456,128]{1,0:T(8,128)}, f32[3456,128]{1,0:T(8,128)}) async-done(((f32[3456,128]{1,0:T(8,128)}, f32[3456,128]{1,0:T(8,128)}), (f32[3456,128]{1,0:T(8,128)}, f32[3456,128]{1,0:T(8,128)})) %all-reduce.88.cloned.1.call-update) | async-done | bytes 3538960 | tf_op jit(solution)/shard_map/psum | solution.py:137
  538.8 3.0 broadcast_multiply_fusion.1
  (232 shorter events, 125.0 us)
Async XLA Ops:
  7.2 153.9 %copy-start = (bf16[3456,128]{1,0:T(8,128)(2,1)S(1)}, bf16[3456,128]{1,0:T(8,128)(2,1)}, u32[]{:S(2)}) copy-start(bf16[3456,128]{1,0:T(8,128)(2,1)} %param.12) | copy-start | bytes 2654212
  8.2 22.2 %copy-start.17 = (s32[8]{0:T(128)}, s32[8]{0:T(128)S(1)}, u32[]{:S(2)}) copy-start(s32[8]{0:T(128)S(1)} %compare_select_fusion.4) | copy-start | bytes 100
  9.6 22.9 %all-to-all-start = ((bf16[32,1,2]{2,1,0:T(2,128)(2,1)}), bf16[32,1,2]{2,1,0:T(2,128)(2,1)S(1)}, u32[]{:S(2)}, u32[]{:S(2)}) async-start(bf16[32,1,2]{2,1,0:T(2,128)(2,1)} %all_to_all.16), calls=%async_computation | async-start | bytes 32768 | tf_op jit(solution)/shard_map/all_to_all | solution.py:86
  29.1 16.1 %copy-start.12 = (s32[8,27]{1,0:T(8,128)S(1)}, s32[8,27]{1,0:T(8,128)}, u32[]{:S(2)}) copy-start(s32[8,27]{1,0:T(8,128)} %param.9) | copy-start | bytes 2596
  32.5 62.9 %all-to-all-start.1 = ((bf16[32,2,64,128]{3,2,1,0:T(8,128)(2,1)}), bf16[32,2,64,128]{3,2,1,0:T(8,128)(2,1)}, u32[]{:S(2)}, u32[]{:S(2)}) async-start(bf16[32,2,64,128]{3,2,1,0:T(8,128)(2,1)} %bitcast.161), calls=%async_computation.1 | async-start | bytes 2097152 | tf_op jit(solution)/shard_map/all_to_all | solution.py:85
  42.4 496.4 %all-reduce.88.cloned.1.call-start = ((), (), s32[]{:S(2)}) async-start(), calls=%async_computation.3 | async-start | bytes 7077888 | tf_op jit(solution)/shard_map/psum | solution.py:137
  53.7 23.4 %copy-start.13 = (s32[216,1]{0,1:T(1,128)}, s32[216,1]{0,1:T(1,128)S(1)}, u32[]{:S(2)}) copy-start(s32[216,1]{0,1:T(1,128)S(1)} %compare_select_fusion.1) | copy-start | bytes 2596
  53.8 27.9 %copy-start.19 = (s32[4]{0:T(128)S(1)}, s32[4]{0:T(128)}, u32[]{:S(2)}) copy-start(s32[4]{0:T(128)} %param.10) | copy-start | bytes 52
  77.2 5.8 %collective-permute-start.9 = (bf16[1,1,4,4,64,128]{5,4,3,2,1,0:T(8,128)(2,1)S(1)}, bf16[1,1,4,4,64,128]{5,4,3,2,1,0:T(8,128)(2,1)S(1)}, u32[]{:S(2)}, u32[]{:S(2)}) collective-permute-start(bf16[1,1,4,4,64,128]{5,4,3,2,1,0:T(8,128)(2,1)S(1)} %bitcast.162), channel_id=1, source_target_pairs={{32,0},{64,32},{96,64},{128,96},{160,128},{192,160},{224,192},{33,... | collective-permute-start | bytes 786440 | tf_op jit(solution)/shard_map/ppermute | solution.py:21
  79.2 7.7 %collective-permute-start.8 = (bf16[1,1,4,4,64,128]{5,4,3,2,1,0:T(8,128)(2,1)S(1)}, bf16[1,1,4,4,64,128]{5,4,3,2,1,0:T(8,128)(2,1)S(1)}, u32[]{:S(2)}, u32[]{:S(2)}) collective-permute-start(bf16[1,1,4,4,64,128]{5,4,3,2,1,0:T(8,128)(2,1)S(1)} %bitcast.163), channel_id=1, source_target_pairs={{0,32},{32,64},{64,96},{96,128},{128,160},{160,192},{192,224},{1,3... | collective-permute-start | bytes 786440 | tf_op jit(solution)/shard_map/ppermute | solution.py:19
  81.7 13.7 %copy-start.15 = (s32[4]{0:T(128)}, s32[4]{0:T(128)S(1)}, u32[]{:S(2)}) copy-start(s32[4]{0:T(128)S(1)} %compare_select_fusion.2) | copy-start | bytes 52
  87.8 20.7 %collective-permute-start.11 = (bf16[3,1,4,4,64,128]{5,4,3,2,1,0:T(8,128)(2,1)}, bf16[3,1,4,4,64,128]{5,4,3,2,1,0:T(8,128)(2,1)S(1)}, u32[]{:S(2)}, u32[]{:S(2)}) collective-permute-start(bf16[3,1,4,4,64,128]{5,4,3,2,1,0:T(8,128)(2,1)} %pad_maximum_fusion.4), channel_id=1, source_target_pairs={{1,0},{2,1},{3,2},{4,3},{5,4},{6,5},{7,6},{8,7},{9,8},{10,9},{11,1... | collective-permute-start | bytes 2359304 | tf_op jit(solution)/shard_map/ppermute | solution.py:21
  89.1 20.7 %collective-permute-start.10 = (bf16[3,1,4,4,64,128]{5,4,3,2,1,0:T(8,128)(2,1)}, bf16[3,1,4,4,64,128]{5,4,3,2,1,0:T(8,128)(2,1)}, u32[]{:S(2)}, u32[]{:S(2)}) collective-permute-start(bf16[3,1,4,4,64,128]{5,4,3,2,1,0:T(8,128)(2,1)} %pad_maximum_fusion.4), channel_id=1, source_target_pairs={{0,1},{1,2},{2,3},{3,4},{4,5},{5,6},{6,7},{7,8},{8,9},{9,10},{10,1... | collective-permute-start | bytes 2359304 | tf_op jit(solution)/shard_map/ppermute | solution.py:19
  95.4 26.6 %copy-start.11 = (s32[1024]{0:T(1024)S(1)}, s32[1024]{0:T(1024)}, u32[]{:S(2)}) copy-start(s32[1024]{0:T(1024)} %pad_clamp_fusion.2) | copy-start | bytes 12292
  101.8 23.0 %copy-start.6 = (bf16[8,64,128]{2,1,0:T(8,128)(2,1)}, bf16[8,64,128]{2,1,0:T(8,128)(2,1)S(1)}, u32[]{:S(2)}) copy-start(bf16[8,64,128]{2,1,0:T(8,128)(2,1)S(1)} %get-tuple-element.92) | copy-start | bytes 393220
  103.0 8.5 %collective-permute-start.1 = (bf16[1,1,4,64,128]{4,3,2,1,0:T(8,128)(2,1)}, bf16[1,1,4,64,128]{4,3,2,1,0:T(8,128)(2,1)S(1)}, u32[]{:S(2)}, u32[]{:S(2)}) collective-permute-start(bf16[1,1,4,64,128]{4,3,2,1,0:T(8,128)(2,1)} %bitcast.4), channel_id=1, source_target_pairs={{32,0},{64,32},{96,64},{128,96},{160,128},{192,160},{224,192},{33,... | collective-permute-start | bytes 196616 | tf_op jit(solution)/shard_map/ppermute | solution.py:21
  104.9 6.6 %collective-permute-start = (bf16[1,1,4,64,128]{4,3,2,1,0:T(8,128)(2,1)}, bf16[1,1,4,64,128]{4,3,2,1,0:T(8,128)(2,1)S(1)}, u32[]{:S(2)}, u32[]{:S(2)}) collective-permute-start(bf16[1,1,4,64,128]{4,3,2,1,0:T(8,128)(2,1)} %bitcast.4), channel_id=1, source_target_pairs={{0,32},{32,64},{64,96},{96,128},{128,160},{160,192},{192,224},{1,3... | collective-permute-start | bytes 196616 | tf_op jit(solution)/shard_map/ppermute | solution.py:19
  112.4 9.5 %collective-permute-start.3 = (bf16[3,1,4,64,128]{4,3,2,1,0:T(8,128)(2,1)S(1)}, bf16[3,1,4,64,128]{4,3,2,1,0:T(8,128)(2,1)S(1)}, u32[]{:S(2)}, u32[]{:S(2)}) collective-permute-start(bf16[3,1,4,64,128]{4,3,2,1,0:T(8,128)(2,1)S(1)} %pad_maximum_fusion.6), channel_id=1, source_target_pairs={{1,0},{2,1},{3,2},{4,3},{5,4},{6,5},{7,6},{8,7},{9,8},{10,9},{11,1... | collective-permute-start | bytes 589832 | tf_op jit(solution)/shard_map/ppermute | solution.py:21
  113.7 8.2 %collective-permute-start.2 = (bf16[3,1,4,64,128]{4,3,2,1,0:T(8,128)(2,1)S(1)}, bf16[3,1,4,64,128]{4,3,2,1,0:T(8,128)(2,1)S(1)}, u32[]{:S(2)}, u32[]{:S(2)}) collective-permute-start(bf16[3,1,4,64,128]{4,3,2,1,0:T(8,128)(2,1)S(1)} %pad_maximum_fusion.6), channel_id=1, source_target_pairs={{0,1},{1,2},{2,3},{3,4},{4,5},{5,6},{6,7},{7,8},{8,9},{9,10},{10,1... | collective-permute-start | bytes 589832 | tf_op jit(solution)/shard_map/ppermute | solution.py:19
  164.8 36.2 %collective-permute-start.5 = (bf16[1,1,4,64,128]{4,3,2,1,0:T(8,128)(2,1)S(1)}, bf16[1,1,4,64,128]{4,3,2,1,0:T(8,128)(2,1)S(1)}, u32[]{:S(2)}, u32[]{:S(2)}) collective-permute-start(bf16[1,1,4,64,128]{4,3,2,1,0:T(8,128)(2,1)S(1)} %bitcast.176), channel_id=1, source_target_pairs={{32,0},{64,32},{96,64},{128,96},{160,128},{192,160},{224,192},{33,... | collective-permute-start | bytes 196616 | tf_op jit(solution)/shard_map/ppermute | solution.py:21
  166.7 34.2 %collective-permute-start.4 = (bf16[1,1,4,64,128]{4,3,2,1,0:T(8,128)(2,1)S(1)}, bf16[1,1,4,64,128]{4,3,2,1,0:T(8,128)(2,1)S(1)}, u32[]{:S(2)}, u32[]{:S(2)}) collective-permute-start(bf16[1,1,4,64,128]{4,3,2,1,0:T(8,128)(2,1)S(1)} %bitcast.177), channel_id=1, source_target_pairs={{0,32},{32,64},{64,96},{96,128},{128,160},{160,192},{192,224},{1,3... | collective-permute-start | bytes 196616 | tf_op jit(solution)/shard_map/ppermute | solution.py:19
  201.0 11.5 %collective-permute-start.7 = (bf16[3,1,4,64,128]{4,3,2,1,0:T(8,128)(2,1)S(1)}, bf16[3,1,4,64,128]{4,3,2,1,0:T(8,128)(2,1)S(1)}, u32[]{:S(2)}, u32[]{:S(2)}) collective-permute-start(bf16[3,1,4,64,128]{4,3,2,1,0:T(8,128)(2,1)S(1)} %pad_maximum_fusion.7), channel_id=1, source_target_pairs={{1,0},{2,1},{3,2},{4,3},{5,4},{6,5},{7,6},{8,7},{9,8},{10,9},{11,1... | collective-permute-start | bytes 589832 | tf_op jit(solution)/shard_map/ppermute | solution.py:21
  202.3 10.1 %collective-permute-start.6 = (bf16[3,1,4,64,128]{4,3,2,1,0:T(8,128)(2,1)S(1)}, bf16[3,1,4,64,128]{4,3,2,1,0:T(8,128)(2,1)S(1)}, u32[]{:S(2)}, u32[]{:S(2)}) collective-permute-start(bf16[3,1,4,64,128]{4,3,2,1,0:T(8,128)(2,1)S(1)} %pad_maximum_fusion.7), channel_id=1, source_target_pairs={{0,1},{1,2},{2,3},{3,4},{4,5},{5,6},{6,7},{7,8},{8,9},{9,10},{10,1... | collective-permute-start | bytes 589832 | tf_op jit(solution)/shard_map/ppermute | solution.py:19
  265.2 39.8 %copy-start.18 = (s32[8]{0:T(128)S(1)}, s32[8]{0:T(128)}, u32[]{:S(2)}) copy-start(s32[8]{0:T(128)} %copy-done.17) | copy-start | bytes 100
  288.8 33.5 %copy-start.16 = (s32[4]{0:T(128)S(1)}, s32[4]{0:T(128)}, u32[]{:S(2)}) copy-start(s32[4]{0:T(128)} %copy-done.15) | copy-start | bytes 52
  288.9 5.9 %collective-permute-start.13 = (bf16[1,1,4,4,64,128]{5,4,3,2,1,0:T(8,128)(2,1)S(1)}, bf16[1,1,4,4,64,128]{5,4,3,2,1,0:T(8,128)(2,1)S(1)}, u32[]{:S(2)}, u32[]{:S(2)}) collective-permute-start(bf16[1,1,4,4,64,128]{5,4,3,2,1,0:T(8,128)(2,1)S(1)} %bitcast.166), channel_id=1, source_target_pairs={{32,0},{64,32},{96,64},{128,96},{160,128},{192,160},{224,192},{33,... | collective-permute-start | bytes 786440 | tf_op jit(solution)/shard_map/ppermute | solution.py:21
  290.8 8.0 %collective-permute-start.12 = (bf16[1,1,4,4,64,128]{5,4,3,2,1,0:T(8,128)(2,1)S(1)}, bf16[1,1,4,4,64,128]{5,4,3,2,1,0:T(8,128)(2,1)S(1)}, u32[]{:S(2)}, u32[]{:S(2)}) collective-permute-start(bf16[1,1,4,4,64,128]{5,4,3,2,1,0:T(8,128)(2,1)S(1)} %bitcast.167), channel_id=1, source_target_pairs={{0,32},{32,64},{64,96},{96,128},{128,160},{160,192},{192,224},{1,3... | collective-permute-start | bytes 786440 | tf_op jit(solution)/shard_map/ppermute | solution.py:19
  298.9 22.8 %collective-permute-start.15 = (bf16[3,1,4,4,64,128]{5,4,3,2,1,0:T(8,128)(2,1)S(1)}, bf16[3,1,4,4,64,128]{5,4,3,2,1,0:T(8,128)(2,1)S(1)}, u32[]{:S(2)}, u32[]{:S(2)}) collective-permute-start(bf16[3,1,4,4,64,128]{5,4,3,2,1,0:T(8,128)(2,1)S(1)} %pad_maximum_fusion.5), channel_id=1, source_target_pairs={{1,0},{2,1},{3,2},{4,3},{5,4},{6,5},{7,6},{8,7},{9,8},{10,9},{11,1... | collective-permute-start | bytes 2359304 | tf_op jit(solution)/shard_map/ppermute | solution.py:21
  300.2 22.0 %collective-permute-start.14 = (bf16[3,1,4,4,64,128]{5,4,3,2,1,0:T(8,128)(2,1)S(1)}, bf16[3,1,4,4,64,128]{5,4,3,2,1,0:T(8,128)(2,1)S(1)}, u32[]{:S(2)}, u32[]{:S(2)}) collective-permute-start(bf16[3,1,4,4,64,128]{5,4,3,2,1,0:T(8,128)(2,1)S(1)} %pad_maximum_fusion.5), channel_id=1, source_target_pairs={{0,1},{1,2},{2,3},{3,4},{4,5},{5,6},{6,7},{7,8},{8,9},{9,10},{10,1... | collective-permute-start | bytes 2359304 | tf_op jit(solution)/shard_map/ppermute | solution.py:19
  305.1 43.8 %copy-start.5 = (bf16[3456,128]{1,0:T(8,128)(2,1)S(1)}, bf16[3456,128]{1,0:T(8,128)(2,1)}, u32[]{:S(2)}) copy-start(bf16[3456,128]{1,0:T(8,128)(2,1)} %param.13) | copy-start | bytes 2654212
  305.1 43.8 %copy-start.7 = (bf16[8,64,128]{2,1,0:T(8,128)(2,1)S(1)}, bf16[8,64,128]{2,1,0:T(8,128)(2,1)}, u32[]{:S(2)}) copy-start(bf16[8,64,128]{2,1,0:T(8,128)(2,1)} %copy-done.6) | copy-start | bytes 393220
  324.7 218.4 %all-to-all-start.2 = ((bf16[32,2,64,128]{3,2,1,0:T(8,128)(2,1)}), bf16[32,2,64,128]{3,2,1,0:T(8,128)(2,1)S(1)}, u32[]{:S(2)}, u32[]{:S(2)}) async-start(bf16[32,2,64,128]{3,2,1,0:T(8,128)(2,1)} %bitcast.65), calls=%async_computation.2 | async-start | bytes 2097152 | tf_op jit(solution)/shard_map/all_to_all | solution.py:135
  (8 other events, 37.3 us)
Sparse Core Ops, SparseCore 0:
  256.4 282.3 all-reduce.87
where the time goes:
time: 562 us; the launch traced here: 551 us
  waiting for transfers between devices  224 us (40%)
  other arithmetic  104 us (19%)
  local copies, waits for them, and re-layouts  96.9 us (17%)
  starting transfers between devices  88.8 us (16%)
  matrix products  21.8 us (4%)
  between operations  15.3 us (3%)
    psum x1, waiting for transfers between devices, per_device(): summed = lax.psum((grad_one, grad_two), ('tile', 'dev'))  186 us
    scatter-add x2, other arithmetic, adjoint(): total.at[neighbours.reshape(-1)]  46.9 us
    ppermute x8, starting transfers between devices, with_halo(): lax.ppermute(tail, axis, [(i, (i + 1) % count) for i in range(ends)])  30.4 us
    unnamed x34, other arithmetic  28.2 us
    all_to_all x1, starting transfers between devices, per_device(): lax.all_to_all(returning, 'dev', split_axis=0, concat_axis=0, tiled=True)  24.2 us
    reshape x3, local copies, waits for them, and re-layouts, patch_columns(): jnp.concatenate(pieces, axis=-1).reshape(count * EDGE ** 3, 27 * channels)  22 us
    ppermute x8, waiting for transfers between devices, with_halo(): lax.ppermute(head, axis, [((i + 1) % count, i) for i in range(ends)])  20.6 us
    ppermute x8, waiting for transfers between devices, with_halo(): lax.ppermute(tail, axis, [(i, (i + 1) % count) for i in range(ends)])  17.7 us
  transfers between devices with their start and end apart: 20, of which 11 were waited for; matrix products, arithmetic and copies ran while one was open for 24% of the time, Pallas kernels for 0%

commit v1 on v0

v1 whole, which is shorter than its diff:
```python
import functools
import math

import jax
import jax.numpy as jnp
import numpy as np
from jax import lax
from jax.experimental import pallas as pl
from jax.experimental.pallas import tpu as pltpu
from jax.sharding import PartitionSpec as P

EDGE = 4
PLANE = EDGE * EDGE
BLK = 8
VOX = 64
CH = 128
RIM = 4
HALF = 27 * CH // 2
QUARTER = HALF // 4
TILES = QUARTER // 16
F32 = jnp.float32
BF16 = jnp.bfloat16
I32 = jnp.int32


def shift_matrix():
    result = np.zeros((9 * PLANE, 9 * PLANE), np.float32)
    for ky in range(3):
        for kz in range(3):
            for j in range(EDGE):
                for k in range(EDGE):
                    y, z = j + ky - 1, k + kz - 1
                    dy, dz = y // EDGE + 1, z // EDGE + 1
                    source = ((dy * 3 + dz) * EDGE + y % EDGE) * EDGE + z % EDGE
                    result[((ky * 3 + kz) * EDGE + j) * EDGE + k, source] = 1.0
    return result


def dot(left, right):
    return jnp.dot(left, right, preferred_element_type=F32)


def unit_kernel(
    n_tile,
    n_dev,
    scale,
    pos,
    nbr,
    rim,
    feat,
    cot,
    w1,
    w2,
    smat,
    out_output,
    out_grad,
    out_sums,
    idxv,
    idxs,
    slotv,
    slots,
    labels,
    packed,
    arrived,
    repacked,
    returned,
    tab_m,
    tab_c,
    tab_h,
    tab_p,
    own,
    rims,
    wt1,
    wt2,
    planes,
    y_m,
    y_c,
    y_x,
    pre_one,
    hidden_grad,
    grads,
    core_in,
    x_out,
    x_in,
    own_sum,
    z_out,
    z_in,
    final,
    sem_local,
    sem_a2a,
    sem_lab,
    sem_back,
    sem_halo_s,
    sem_halo_r,
    sem_sum_s,
    sem_sum_r,
):
    tile = lax.axis_index("tile")
    dev = lax.axis_index("dev")
    core = lax.rem(tile, 2)
    chip_x = tile // 2
    n_x = n_tile // 2

    def remote(src, dst, send, recv, **where):
        return pltpu.make_async_remote_copy(
            src_ref=src,
            dst_ref=dst,
            send_sem=send,
            recv_sem=recv,
            device_id=where,
            device_id_type=pl.DeviceIdType.MESH,
        )

    def await_bytes(ref, sem):
        pltpu.make_async_copy(ref, ref, sem).wait()

    barrier = pltpu.get_barrier_semaphore()

    @pl.loop(1, n_dev)
    def _(d):
        pl.semaphore_signal(barrier, inc=1, device_id={"dev": lax.rem(dev + d, n_dev)})

    @pl.loop(1, n_tile)
    def _(d):
        pl.semaphore_signal(barrier, inc=1, device_id={"tile": lax.rem(tile + d, n_tile)})

    sub = lax.broadcasted_iota(I32, (8, CH), 0)
    lane = lax.broadcasted_iota(I32, (8, CH), 1)
    posv = jnp.zeros((8, CH), I32)
    for r in range(BLK):
        posv = jnp.where(sub == r, pos[r], posv)
    owner = posv // BLK
    count = jnp.zeros((8, CH), I32)
    for r in range(BLK):
        count = count + jnp.where((owner == pos[r] // BLK) & (sub > r), 1, 0)
    slot_of_row = lax.rem(owner - dev + n_dev, n_dev) * 2 + count
    hit = lane == slot_of_row
    row_of_slot = jnp.min(jnp.where(hit, sub, BLK - 1), axis=0, keepdims=True)
    label_of_slot = jnp.min(jnp.where(hit, lax.rem(posv, BLK), BLK), axis=0, keepdims=True)
    idxv[0] = jnp.broadcast_to(row_of_slot, (8, CH))
    idxv[1] = jnp.minimum(slot_of_row, 2 * n_dev - 1)
    labels[0] = jnp.broadcast_to(label_of_slot, (8, CH))
    to_scalars = pltpu.make_async_copy(idxv, idxs, sem_local.at[0])
    to_scalars.start()

    def pack_rims(rows, which):
        for h in range(RIM):
            rims[which, h] = rows[rim[h]]

    def halo_copies(which, table):
        result = []
        for q, where in enumerate(
            (
                dict(tile=lax.rem(tile + 1, n_tile)),
                dict(tile=lax.rem(tile + n_tile - 1, n_tile)),
                dict(dev=lax.rem(dev + 1, n_dev)),
                dict(dev=lax.rem(dev + n_dev - 1, n_dev)),
            )
        ):
            result.append(
                remote(
                    rims.at[which],
                    table.at[pl.ds(BLK + q * RIM, RIM)],
                    sem_halo_s.at[which, q],
                    sem_halo_r.at[which, q],
                    **where,
                )
            )
        return result

    def finish_halo(copies, table):
        for copy in copies:
            copy.wait()
        edges = (tile == 0, tile == n_tile - 1, dev == 0, dev == n_dev - 1)
        for q, edge in enumerate(edges):

            @pl.when(edge)
            def _(q=q):
                table[BLK + q * RIM : BLK + (q + 1) * RIM] = jnp.zeros((RIM, VOX, CH), BF16)

    for table in (tab_m, tab_c, tab_h, tab_p):
        table[BLK + 4 * RIM] = jnp.zeros((VOX, CH), BF16)
    tab_c[0:BLK] = cot[...]
    pack_rims(cot, 0)
    to_scalars.wait()

    @pl.loop(0, n_dev)
    def _(d):
        for c in range(2):
            packed[d, c] = feat[idxs[0, 0, 2 * d + c]]

    arrived[0] = packed[0]

    pl.semaphore_wait(barrier, n_dev + n_tile - 2)

    @pl.loop(1, n_dev)
    def _(d):
        where = lax.rem(dev + d, n_dev)
        remote(labels.at[0], labels.at[d], sem_lab.at[0], sem_lab.at[1], dev=where).start()
        remote(packed.at[d], arrived.at[d], sem_a2a.at[0], sem_a2a.at[1], dev=where).start()

    halo_c = halo_copies(0, tab_c)
    for copy in halo_c:
        copy.start()

    def flip_weights(source, target):
        for o in range(27):
            piece = source[o * CH : (o + 1) * CH, :].astype(F32)
            target[(26 - o) * CH : (27 - o) * CH, :] = piece.T.astype(BF16)

    def expand(table, y):
        @pl.loop(0, BLK)
        def _(b):
            for i in range(6):
                dx = 0 if i == 0 else (2 if i == 5 else 1)
                row = (i + EDGE - 1) % EDGE
                for t in range(9):
                    entry = nbr[b, dx * 9 + t]
                    planes[t * PLANE : (t + 1) * PLANE, i * CH : (i + 1) * CH] = table[
                        entry, row * PLANE : (row + 1) * PLANE, :
                    ]
            moved = dot(smat[...], planes[...]).astype(BF16)
            for i in range(6):
                for t in range(9):
                    y[b, i, :, t * CH : (t + 1) * CH] = moved[
                        t * PLANE : (t + 1) * PLANE, i * CH : (i + 1) * CH
                    ]

    def columns(y, kx):
        return y[:, kx : kx + EDGE].reshape(BLK * VOX, 9 * CH)

    def conv(y, w):
        return (
            dot(columns(y, 0), w[0 : 9 * CH, :])
            + dot(columns(y, 1), w[9 * CH : 18 * CH, :])
            + dot(columns(y, 2), w[18 * CH : 27 * CH, :])
        )

    flip_weights(w2, wt2)
    flip_weights(w1, wt1)
    finish_halo(halo_c, tab_c)
    expand(tab_c, y_c)
    hidden_grad[...] = conv(y_c, wt2)

    await_bytes(labels.at[pl.ds(1, n_dev - 1)], sem_lab.at[1])
    label_at = jnp.zeros((8, CH), I32)
    for d in range(n_dev):
        label_at = jnp.where(lane // 2 == d, labels[d], label_at)
    label_at = jnp.where(lane < 2 * n_dev, label_at, BLK)
    slotv[0] = jnp.minimum(label_at, BLK - 1)
    slotv[1] = jnp.broadcast_to(
        jnp.max(jnp.where(label_at == sub, lane, 0), axis=1, keepdims=True), (8, CH)
    )
    to_slots = pltpu.make_async_copy(slotv, slots, sem_local.at[0])
    to_slots.start()
    to_slots.wait()
    await_bytes(arrived.at[pl.ds(1, n_dev - 1)], sem_a2a.at[1])
    for s in range(BLK):
        linear = slots[1, s, 0]
        own[0, s] = arrived[linear // 2, lax.rem(linear, 2)]
    tab_m[0:BLK] = own[0]
    pack_rims(own.at[0], 1)
    halo_m = halo_copies(1, tab_m)
    for copy in halo_m:
        copy.start()
    finish_halo(halo_m, tab_m)
    expand(tab_m, y_m)
    pre = conv(y_m, w1)
    gate = jax.nn.sigmoid(pre)
    hidden = (pre * gate).astype(BF16)
    pre_grad = (hidden_grad[...] * gate * (1.0 + pre * (1.0 - gate))).astype(BF16)
    tab_h[0:BLK] = hidden.reshape(BLK, VOX, CH)
    tab_p[0:BLK] = pre_grad.reshape(BLK, VOX, CH)
    own[1] = hidden.reshape(BLK, VOX, CH)
    own[2] = pre_grad.reshape(BLK, VOX, CH)
    pack_rims(own.at[1], 2)
    pack_rims(own.at[2], 3)
    halo_h = halo_copies(2, tab_h)
    halo_p = halo_copies(3, tab_p)
    for copy in halo_h + halo_p:
        copy.start()

    partner = dict(tile=tile + 1 - 2 * core)

    def half_rows(which):
        return pl.ds(pl.multiple_of(which * HALF, 16), HALF)

    def core_copy(q):
        return remote(
            grads.at[q, half_rows(1 - core)],
            core_in.at[q],
            sem_sum_s.at[q, 0],
            sem_sum_r.at[q, 0],
            **partner,
        )

    hidden_t = own[1].reshape(BLK * VOX, CH).astype(F32).T.astype(BF16)
    for kx in range(3):
        part = dot(hidden_t, columns(y_c, kx))
        for t in range(9):
            o = 26 - (kx * 9 + t)
            grads[1, o * CH : (o + 1) * CH, :] = part[:, t * CH : (t + 1) * CH]
    core_copy(1).start()
    pre_grad_t = own[2].reshape(BLK * VOX, CH).astype(F32).T.astype(BF16)
    for kx in range(3):
        part = dot(pre_grad_t, columns(y_m, kx))
        for t in range(9):
            o = kx * 9 + t
            grads[0, o * CH : (o + 1) * CH, :] = part[:, t * CH : (t + 1) * CH].T
    core_copy(0).start()

    def x_copy(q, e):
        other = lax.rem(chip_x + e, n_x)
        return remote(
            x_out.at[q, other],
            x_in.at[q, e - 1],
            sem_sum_s.at[q, 1],
            sem_sum_r.at[q, 1],
            tile=other * 2 + core,
        )

    def both_cores(q, chunk):
        start = pl.multiple_of(core * HALF + chunk * QUARTER, 16)
        start_in = pl.multiple_of(chunk * QUARTER, 16)
        return grads[q, pl.ds(start, QUARTER), :] + core_in[q, pl.ds(start_in, QUARTER), :]

    def start_x(q):
        core_copy(q).wait_recv()
        for j in range(n_x):
            x_out[q, j] = both_cores(q, j).astype(BF16)
        for e in range(1, n_x):
            x_copy(q, e).start()

    def start_z(q):
        await_bytes(x_in.at[q], sem_sum_r.at[q, 1])
        total = both_cores(q, chip_x)
        for e in range(n_x - 1):
            total = total + x_in[q, e].astype(F32)
        own_sum[q, 0:QUARTER] = total
        own_sum[q, QUARTER:] = jnp.zeros((n_dev * 16 - QUARTER, CH), F32)
        z_out[q, 0:TILES] = total.astype(BF16).reshape(TILES, 16, CH)
        z_out[q, TILES:] = jnp.zeros((n_dev - TILES, 16, CH), BF16)

        @pl.loop(1, n_dev)
        def _(d):
            where = lax.rem(dev + d, n_dev)
            remote(
                z_out.at[q, where], z_in.at[q, d - 1], sem_sum_s.at[q, 2], sem_sum_r.at[q, 2], dev=where
            ).start()

    def start_gather_z(q):
        await_bytes(z_in.at[q], sem_sum_r.at[q, 2])
        total = own_sum[q, pl.ds(pl.multiple_of(dev * 16, 16), 16), :]
        for d in range(n_dev - 1):
            total = total + z_in[q, d].astype(F32)
        final[q, core, chip_x, dev] = (total * scale).astype(BF16)

        @pl.loop(1, n_dev)
        def _(d):
            where = lax.rem(dev + d, n_dev)
            mine = final.at[q, core, chip_x, dev]
            remote(mine, mine, sem_sum_s.at[q, 3], sem_sum_r.at[q, 3], dev=where).start()

    def gather_x_copy(q, e):
        mine = final.at[q, core, chip_x, pl.ds(0, TILES)]
        return remote(
            mine, mine, sem_sum_s.at[q, 4], sem_sum_r.at[q, 4], tile=lax.rem(chip_x + e, n_x) * 2 + core
        )

    def start_gather_x(q):
        await_bytes(z_in.at[q], sem_sum_r.at[q, 3])
        for e in range(1, n_x):
            gather_x_copy(q, e).start()

    def gather_core_copy(q):
        mine = final.at[q, core, :, pl.ds(0, TILES)]
        return remote(mine, mine, sem_sum_s.at[q, 5], sem_sum_r.at[q, 5], **partner)

    def start_gather_core(q):
        await_bytes(x_in.at[q], sem_sum_r.at[q, 4])
        gather_core_copy(q).start()

    start_x(1)
    start_x(0)
    finish_halo(halo_h, tab_h)
    expand(tab_h, y_x)
    pre_two = conv(y_x, w2)
    out_output[...] = (
        (own[0].reshape(BLK * VOX, CH).astype(F32) + pre_two).astype(BF16).reshape(BLK, VOX, CH)
    )
    start_z(1)
    start_z(0)
    finish_halo(halo_p, tab_p)
    expand(tab_p, y_x)
    back = conv(y_x, wt1) + cot[...].reshape(BLK * VOX, CH).astype(F32)
    own[1] = back.astype(BF16).reshape(BLK, VOX, CH)

    @pl.loop(0, n_dev)
    def _(d):
        for c in range(2):
            repacked[d, c] = own[1, slots[0, 0, 2 * d + c]]

    returned[0] = repacked[0]

    @pl.loop(1, n_dev)
    def _(d):
        where = lax.rem(dev - d + n_dev, n_dev)
        remote(repacked.at[d], returned.at[d], sem_back.at[0], sem_back.at[1], dev=where).start()

    start_gather_z(1)
    start_gather_z(0)
    start_gather_x(1)
    start_gather_x(0)
    start_gather_core(1)
    start_gather_core(0)
    await_bytes(returned.at[pl.ds(1, n_dev - 1)], sem_back.at[1])
    for r in range(BLK):
        linear = idxs[1, r, 0]
        out_grad[r] = returned[linear // 2, lax.rem(linear, 2)]
    gather_core_copy(1).wait_recv()
    gather_core_copy(0).wait_recv()
    out_sums[...] = final[...]

    await_bytes(labels.at[pl.ds(1, n_dev - 1)], sem_lab.at[0])
    await_bytes(packed.at[pl.ds(1, n_dev - 1)], sem_a2a.at[0])
    await_bytes(repacked.at[pl.ds(1, n_dev - 1)], sem_back.at[0])
    for q in range(2):
        core_copy(q).wait_send()
        await_bytes(x_in.at[q], sem_sum_s.at[q, 1])
        await_bytes(z_in.at[q], sem_sum_s.at[q, 2])
        await_bytes(z_in.at[q], sem_sum_s.at[q, 3])
        await_bytes(x_in.at[q], sem_sum_s.at[q, 4])
        gather_core_copy(q).wait_send()


def per_device(
    n_tile, n_dev, features, morton_pos, neighbours, rim, cotangent, weight_one, weight_two
):
    blocks, voxels, channels = features.shape
    scale = 1.0 / math.sqrt(blocks * voxels * n_tile * n_dev)
    n_x = n_tile // 2
    smem = pl.BlockSpec(memory_space=pltpu.SMEM)
    vmem = pl.BlockSpec(memory_space=pltpu.VMEM)
    dma = pltpu.SemaphoreType.DMA
    block_table = pltpu.VMEM((BLK + 4 * RIM + 1, VOX, CH), BF16)
    wide = pltpu.VMEM((BLK, 6, PLANE, 9 * CH), BF16)
    flat = pltpu.VMEM((BLK * VOX, CH), F32)
    slab = pltpu.VMEM((n_dev, 2, VOX, CH), BF16)
    output, input_grad, sums = pl.pallas_call(
        functools.partial(unit_kernel, n_tile, n_dev, scale),
        out_shape=(
            jax.ShapeDtypeStruct(features.shape, BF16),
            jax.ShapeDtypeStruct(features.shape, BF16),
            jax.ShapeDtypeStruct((2, 2, n_x, n_dev, 16, CH), BF16),
        ),
        in_specs=[smem, smem, smem, vmem, vmem, vmem, vmem, vmem],
        out_specs=(vmem, vmem, vmem),
        scratch_shapes=[
            pltpu.VMEM((2, 8, CH), I32),
            pltpu.SMEM((2, 8, CH), I32),
            pltpu.VMEM((2, 8, CH), I32),
            pltpu.SMEM((2, 8, CH), I32),
            pltpu.VMEM((n_dev, 8, CH), I32),
            slab,
            slab,
            slab,
            slab,
            block_table,
            block_table,
            block_table,
            block_table,
            pltpu.VMEM((3, BLK, VOX, CH), BF16),
            pltpu.VMEM((4, RIM, VOX, CH), BF16),
            pltpu.VMEM((27 * CH, CH), BF16),
            pltpu.VMEM((27 * CH, CH), BF16),
            pltpu.VMEM((9 * PLANE, 6 * CH), BF16),
            wide,
            wide,
            wide,
            flat,
            flat,
            pltpu.VMEM((2, 27 * CH, CH), F32),
            pltpu.VMEM((2, HALF, CH), F32),
            pltpu.VMEM((2, n_x, QUARTER, CH), BF16),
            pltpu.VMEM((2, n_x - 1, QUARTER, CH), BF16),
            pltpu.VMEM((2, n_dev * 16, CH), F32),
            pltpu.VMEM((2, n_dev, 16, CH), BF16),
            pltpu.VMEM((2, n_dev - 1, 16, CH), BF16),
            pltpu.VMEM((2, 2, n_x, n_dev, 16, CH), BF16),
            dma((1,)),
            dma((2,)),
            dma((2,)),
            dma((2,)),
            dma((4, 4)),
            dma((4, 4)),
            dma((2, 6)),
            dma((2, 6)),
        ],
        compiler_params=pltpu.CompilerParams(
            collective_id=0, has_side_effects=True, vmem_limit_bytes=48 * 1024 * 1024
        ),
    )(
        morton_pos,
        neighbours,
        rim,
        features,
        cotangent,
        weight_one,
        weight_two,
        jnp.asarray(shift_matrix(), BF16),
    )
    kernels = sums[:, :, :, :TILES].astype(F32).reshape(2, 27 * CH, CH)
    return (output, input_grad, kernels[0], kernels[1])


def solution(mesh):
    placed = (
        P(("tile", "dev"), None, None),
        P(("tile", "dev")),
        P(("tile", "dev"), None),
        P(("tile", "dev")),
        P(("tile", "dev"), None, None),
        P(),
        P(),
    )
    return jax.shard_map(
        functools.partial(per_device, mesh.shape["tile"], mesh.shape["dev"]),
        mesh=mesh,
        in_specs=placed,
        out_specs=(P(("tile", "dev"), None, None), P(("tile", "dev"), None, None), P(), P()),
        check_vma=False,
    )
```

time: 562 us -> 129 us (0.23)
  the two profiles are of different devices: /device:TPU:2 before, /device:TPU:1 now
where the time goes in v1:
time: 129 us
  Pallas kernels  117 us (91%)
  local copies, waits for them, and re-layouts  10.3 us (8%)
    pallas_call x1, Pallas kernels, per_device(): pl.pallas_call(functools.partial(unit_kernel, n_tile, n_dev, scale), out_...  117 us
    unnamed x18, local copies, waits for them, and re-layouts  8.32 us

profile of v1, /device:TPU:1, one launch (start us, length us, event | category | flops | bytes accessed | tf_op | source)
XLA Modules:
  0.0 128.5 jit_solution(8025949147743263053)
XLA Ops:
  0.6 0.0 copy-start
  0.6 1.2 copy-done
  1.8 0.0 copy-start.1
  1.8 1.2 copy-done.1
  3.0 0.0 copy-start.2
  3.0 0.9 copy-done.2
  3.9 0.0 copy-start.3
  3.9 0.9 copy-done.3
  4.8 0.0 copy-start.4
  4.8 0.9 copy-done.4
  5.7 0.0 copy-start.5
  5.7 0.7 copy-done.5
  6.4 0.0 copy-start.6
  6.4 0.7 copy-done.6
  7.0 0.0 copy-start.7
  7.0 0.7 copy-done.7
  7.7 117.2 %shard_map.111 = (bf16[8,64,128]{2,1,0:T(8,128)(2,1)S(1)}, bf16[8,64,128]{2,1,0:T(8,128)(2,1)S(1)}, bf16[2,2,4,32,16,128]{5,4,3,2,1,0:T(8,128)(2,1)S(1)}) custom-call(s32[8]{0:T(128)S(1)} %copy-done.6, s32[8,27]{1,0:T(8,128)S(1)} %copy-done.5, s32[4]{0:T(128)S(1)} %copy-done.7, bf16[8,64,128]{2,1,0:T(8,128)(2,1)S(1)} %copy-done.2, ...), custom_call_target="tpu_custom_call" | custom-call | tf_op jit(solution)/shard_map/pallas_call | solution.py:449
  124.9 0.3 slice_convert_fusion
  125.2 2.0 %fusion = (f32[1,2,4,27,16,128]{5,4,3,2,1,0:T(8,128)}, f32[1,2,4,27,16,128]{5,4,3,2,1,0:T(8,128)}) fusion(f32[2,2,4,27,16,128]{5,4,3,2,1,0:T(8,128)S(1)} %slice_convert_fusion), kind=kLoop, calls=%fused_computation.1 | loop fusion | bytes 7077888 | tf_op jit(solution)/shard_map/slice | solution.py:513
  127.2 0.7 copy.14
  127.9 0.7 copy.15
Async XLA Ops:
  0.6 1.2 copy-start
  1.8 1.2 copy-start.1
  3.0 0.9 copy-start.2
  3.9 0.9 copy-start.3
  4.8 0.9 copy-start.4
  5.7 0.7 copy-start.5
  6.4 0.7 copy-start.6
  7.0 0.7 copy-start.7

commit v2 on v1

--- a/solution.py
+++ b/solution.py
@@ -18,6 +18,7 @@
 HALF = 27 * CH // 2
 QUARTER = HALF // 4
 TILES = QUARTER // 16
+PIECE = 7 * 16
 F32 = jnp.float32
 BF16 = jnp.bfloat16
 I32 = jnp.int32
@@ -44,6 +45,17 @@
     n_tile,
     n_dev,
     scale,
+    pos_in,
+    nbr_in,
+    rim_in,
+    feat_in,
+    cot_in,
+    w1_in,
+    w2_in,
+    smat_in,
+    out_output,
+    out_grad,
+    out_sums,
     pos,
     nbr,
     rim,
@@ -52,9 +64,6 @@
     w1,
     w2,
     smat,
-    out_output,
-    out_grad,
-    out_sums,
     idxv,
     idxs,
     slotv,
@@ -82,10 +91,13 @@
     core_in,
     x_out,
     x_in,
+    y_out,
+    y_in,
     own_sum,
     z_out,
     z_in,
     final,
+    sem_in,
     sem_local,
     sem_a2a,
     sem_lab,
@@ -94,6 +106,7 @@
     sem_halo_r,
     sem_sum_s,
     sem_sum_r,
+    sem_first,
 ):
     tile = lax.axis_index("tile")
     dev = lax.axis_index("dev")
@@ -114,6 +127,15 @@
     def await_bytes(ref, sem):
         pltpu.make_async_copy(ref, ref, sem).wait()
 
+    operands = (pos_in, rim_in, feat_in, cot_in, w2_in, w1_in, smat_in, nbr_in)
+    places = (pos, rim, feat, cot, w2, w1, smat, nbr)
+    loads = [
+        pltpu.make_async_copy(source, place, sem_in.at[i])
+        for i, (source, place) in enumerate(zip(operands, places))
+    ]
+    load_pos, load_rim, load_feat, load_cot, load_w2, load_w1, load_smat, load_nbr = loads
+    for load in loads:
+        load.start()
     barrier = pltpu.get_barrier_semaphore()
 
     @pl.loop(1, n_dev)
@@ -126,6 +148,7 @@
 
     sub = lax.broadcasted_iota(I32, (8, CH), 0)
     lane = lax.broadcasted_iota(I32, (8, CH), 1)
+    load_pos.wait()
     posv = jnp.zeros((8, CH), I32)
     for r in range(BLK):
         posv = jnp.where(sub == r, pos[r], posv)
@@ -180,8 +203,11 @@
 
     for table in (tab_m, tab_c, tab_h, tab_p):
         table[BLK + 4 * RIM] = jnp.zeros((VOX, CH), BF16)
+    load_rim.wait()
+    load_cot.wait()
     tab_c[0:BLK] = cot[...]
     pack_rims(cot, 0)
+    load_feat.wait()
     to_scalars.wait()
 
     @pl.loop(0, n_dev)
@@ -236,8 +262,12 @@
             + dot(columns(y, 2), w[18 * CH : 27 * CH, :])
         )
 
+    load_w2.wait()
     flip_weights(w2, wt2)
+    load_w1.wait()
     flip_weights(w1, wt1)
+    load_smat.wait()
+    load_nbr.wait()
     finish_halo(halo_c, tab_c)
     expand(tab_c, y_c)
     hidden_grad[...] = conv(y_c, wt2)
@@ -309,87 +339,110 @@
             grads[0, o * CH : (o + 1) * CH, :] = part[:, t * CH : (t + 1) * CH].T
     core_copy(0).start()
 
-    def x_copy(q, e):
-        other = lax.rem(chip_x + e, n_x)
-        return remote(
-            x_out.at[q, other],
-            x_in.at[q, e - 1],
-            sem_sum_s.at[q, 1],
-            sem_sum_r.at[q, 1],
-            tile=other * 2 + core,
-        )
+    y = lax.rem(dev, 4)
+    z = dev // 4
+    n_z = n_dev // 4
+
+    def peer(dim, e):
+        if dim == "x":
+            other = lax.rem(chip_x + e, n_x)
+            return other, dict(tile=other * 2 + core)
+        if dim == "y":
+            other = lax.rem(y + e, 4)
+            return other, dict(dev=z * 4 + other)
+        other = lax.rem(z + e, n_z)
+        return other, dict(dev=other * 4 + y)
+
+    dims = (("x", "y"), ("y", "x"))
+    place = dict(x=chip_x, y=y)
+
+    def sem(q, stage):
+        return sem_sum_s.at[q, stage], sem_sum_r.at[q, stage]
 
     def both_cores(q, chunk):
         start = pl.multiple_of(core * HALF + chunk * QUARTER, 16)
         start_in = pl.multiple_of(chunk * QUARTER, 16)
         return grads[q, pl.ds(start, QUARTER), :] + core_in[q, pl.ds(start_in, QUARTER), :]
 
-    def start_x(q):
+    def start_first(q):
         core_copy(q).wait_recv()
-        for j in range(n_x):
+        for j in range(4):
             x_out[q, j] = both_cores(q, j).astype(BF16)
-        for e in range(1, n_x):
-            x_copy(q, e).start()
-
-    def start_z(q):
+        for e in (2, 1, 3):
+            other, where = peer(dims[q][0], e)
+            remote(x_out.at[q, other], x_in.at[q, e - 1], *sem(q, 1), **where).start()
+
+    def start_second(q):
         await_bytes(x_in.at[q], sem_sum_r.at[q, 1])
-        total = both_cores(q, chip_x)
-        for e in range(n_x - 1):
+        total = both_cores(q, place[dims[q][0]])
+        for e in range(3):
             total = total + x_in[q, e].astype(F32)
         own_sum[q, 0:QUARTER] = total
-        own_sum[q, QUARTER:] = jnp.zeros((n_dev * 16 - QUARTER, CH), F32)
-        z_out[q, 0:TILES] = total.astype(BF16).reshape(TILES, 16, CH)
-        z_out[q, TILES:] = jnp.zeros((n_dev - TILES, 16, CH), BF16)
-
-        @pl.loop(1, n_dev)
-        def _(d):
-            where = lax.rem(dev + d, n_dev)
-            remote(
-                z_out.at[q, where], z_in.at[q, d - 1], sem_sum_s.at[q, 2], sem_sum_r.at[q, 2], dev=where
-            ).start()
-
-    def start_gather_z(q):
-        await_bytes(z_in.at[q], sem_sum_r.at[q, 2])
-        total = own_sum[q, pl.ds(pl.multiple_of(dev * 16, 16), 16), :]
-        for d in range(n_dev - 1):
-            total = total + z_in[q, d].astype(F32)
-        final[q, core, chip_x, dev] = (total * scale).astype(BF16)
-
-        @pl.loop(1, n_dev)
-        def _(d):
-            where = lax.rem(dev + d, n_dev)
-            mine = final.at[q, core, chip_x, dev]
-            remote(mine, mine, sem_sum_s.at[q, 3], sem_sum_r.at[q, 3], dev=where).start()
-
-    def gather_x_copy(q, e):
-        mine = final.at[q, core, chip_x, pl.ds(0, TILES)]
-        return remote(
-            mine, mine, sem_sum_s.at[q, 4], sem_sum_r.at[q, 4], tile=lax.rem(chip_x + e, n_x) * 2 + core
-        )
-
-    def start_gather_x(q):
+        own_sum[q, QUARTER:] = jnp.zeros((4 * PIECE - QUARTER, CH), F32)
+        for j in range(4):
+            y_out[q, j] = own_sum[q, j * PIECE : (j + 1) * PIECE].astype(BF16)
+        for e in (2, 1, 3):
+            other, where = peer(dims[q][1], e)
+            remote(y_out.at[q, other], y_in.at[q, e - 1], *sem(q, 2), **where).start()
+
+    def start_third(q):
+        await_bytes(y_in.at[q], sem_sum_r.at[q, 2])
+        start = pl.multiple_of(place[dims[q][1]] * PIECE, 16)
+        total = own_sum[q, pl.ds(start, PIECE), :]
+        for e in range(3):
+            total = total + y_in[q, e].astype(F32)
+        z_out[q, 0:7] = total.reshape(7, 16, CH)
+        z_out[q, 7] = jnp.zeros((16, CH), F32)
+        for e in (4, 3, 5, 2, 6, 1, 7):
+            other, where = peer("z", e)
+            remote(z_out.at[q, other], z_in.at[q, e - 1], *sem(q, 3), **where).start()
+
+    def start_gather_third(q):
         await_bytes(z_in.at[q], sem_sum_r.at[q, 3])
-        for e in range(1, n_x):
-            gather_x_copy(q, e).start()
-
-    def gather_core_copy(q):
-        mine = final.at[q, core, :, pl.ds(0, TILES)]
-        return remote(mine, mine, sem_sum_s.at[q, 5], sem_sum_r.at[q, 5], **partner)
+        total = z_out[q, z]
+        for e in range(7):
+            total = total + z_in[q, e]
+        mine = final.at[q, core, place[dims[q][0]], place[dims[q][1]], z]
+        mine[...] = (total * scale).astype(BF16)
+        for e in (4, 3, 5, 2, 6, 1, 7):
+            _, where = peer("z", e)
+            remote(mine, mine, *sem(q, 4), **where).start()
+
+    def start_gather_second(q):
+        await_bytes(final.at[q, core, 0, 0, pl.ds(0, 7)], sem_sum_r.at[q, 4])
+        mine = final.at[q, core, place[dims[q][0]], place[dims[q][1]], pl.ds(0, 7)]
+        for e in (2, 1, 3):
+            _, where = peer(dims[q][1], e)
+            remote(mine, mine, *sem(q, 5), **where).start()
+
+    def gather_core_copy(q, chunk):
+        piece = final.at[q, core, chunk, :, pl.ds(0, 7)]
+        return remote(piece, piece, *sem(q, 7), **partner)
+
+    def gather_first_copy(q, e):
+        mine = final.at[q, core, place[dims[q][0]], :, pl.ds(0, 7)]
+        _, where = peer(dims[q][0], e)
+        return remote(mine, mine, sem_sum_s.at[q, 6], sem_first.at[q, e - 1], **where)
+
+    def start_gather_first(q):
+        await_bytes(final.at[q, core, 0, pl.ds(0, 3), pl.ds(0, 7)], sem_sum_r.at[q, 5])
+        for e in (2, 1, 3):
+            gather_first_copy(q, e).start()
+        gather_core_copy(q, place[dims[q][0]]).start()
 
     def start_gather_core(q):
-        await_bytes(x_in.at[q], sem_sum_r.at[q, 4])
-        gather_core_copy(q).start()
-
-    start_x(1)
-    start_x(0)
+        for e in (1, 3, 2):
+            gather_first_copy(q, e).wait_recv()
+            gather_core_copy(q, lax.rem(place[dims[q][0]] + 4 - e, 4)).start()
+
+    start_first(1)
+    start_first(0)
     finish_halo(halo_h, tab_h)
     expand(tab_h, y_x)
     pre_two = conv(y_x, w2)
     out_output[...] = (
         (own[0].reshape(BLK * VOX, CH).astype(F32) + pre_two).astype(BF16).reshape(BLK, VOX, CH)
     )
-    start_z(1)
-    start_z(0)
     finish_halo(halo_p, tab_p)
     expand(tab_p, y_x)
     back = conv(y_x, wt1) + cot[...].reshape(BLK * VOX, CH).astype(F32)
@@ -407,30 +460,38 @@
         where = lax.rem(dev - d + n_dev, n_dev)
         remote(repacked.at[d], returned.at[d], sem_back.at[0], sem_back.at[1], dev=where).start()
 
-    start_gather_z(1)
-    start_gather_z(0)
-    start_gather_x(1)
-    start_gather_x(0)
-    start_gather_core(1)
-    start_gather_core(0)
+    for stage in (
+        start_second,
+        start_third,
+        start_gather_third,
+        start_gather_second,
+        start_gather_first,
+        start_gather_core,
+    ):
+        stage(1)
+        stage(0)
     await_bytes(returned.at[pl.ds(1, n_dev - 1)], sem_back.at[1])
     for r in range(BLK):
         linear = idxs[1, r, 0]
         out_grad[r] = returned[linear // 2, lax.rem(linear, 2)]
-    gather_core_copy(1).wait_recv()
-    gather_core_copy(0).wait_recv()
-    out_sums[...] = final[...]
 
     await_bytes(labels.at[pl.ds(1, n_dev - 1)], sem_lab.at[0])
     await_bytes(packed.at[pl.ds(1, n_dev - 1)], sem_a2a.at[0])
     await_bytes(repacked.at[pl.ds(1, n_dev - 1)], sem_back.at[0])
     for q in range(2):
+        await_bytes(final.at[q, 1 - core, :, :, pl.ds(0, 7)], sem_sum_r.at[q, 7])
+        for c in range(2):
+            for j in range(4):
+                out_sums[q, c, j] = final[q, c, j, :, 0:7].reshape(28, 16, CH)[0:TILES]
+    for q in range(2):
         core_copy(q).wait_send()
         await_bytes(x_in.at[q], sem_sum_s.at[q, 1])
-        await_bytes(z_in.at[q], sem_sum_s.at[q, 2])
+        await_bytes(y_in.at[q], sem_sum_s.at[q, 2])
         await_bytes(z_in.at[q], sem_sum_s.at[q, 3])
-        await_bytes(x_in.at[q], sem_sum_s.at[q, 4])
-        gather_core_copy(q).wait_send()
+        await_bytes(final.at[q, core, 0, 0, pl.ds(0, 7)], sem_sum_s.at[q, 4])
+        await_bytes(final.at[q, core, 0, pl.ds(0, 3), pl.ds(0, 7)], sem_sum_s.at[q, 5])
+        await_bytes(final.at[q, core, pl.ds(0, 3), :, pl.ds(0, 7)], sem_sum_s.at[q, 6])
+        await_bytes(final.at[q, core, :, :, pl.ds(0, 7)], sem_sum_s.at[q, 7])
 
 
 def per_device(
@@ -439,7 +500,7 @@
     blocks, voxels, channels = features.shape
     scale = 1.0 / math.sqrt(blocks * voxels * n_tile * n_dev)
     n_x = n_tile // 2
-    smem = pl.BlockSpec(memory_space=pltpu.SMEM)
+    hbm = pl.BlockSpec(memory_space=pltpu.HBM)
     vmem = pl.BlockSpec(memory_space=pltpu.VMEM)
     dma = pltpu.SemaphoreType.DMA
     block_table = pltpu.VMEM((BLK + 4 * RIM + 1, VOX, CH), BF16)
@@ -451,11 +512,19 @@
         out_shape=(
             jax.ShapeDtypeStruct(features.shape, BF16),
             jax.ShapeDtypeStruct(features.shape, BF16),
-            jax.ShapeDtypeStruct((2, 2, n_x, n_dev, 16, CH), BF16),
+            jax.ShapeDtypeStruct((2, 2, 4, TILES, 16, CH), BF16),
         ),
-        in_specs=[smem, smem, smem, vmem, vmem, vmem, vmem, vmem],
+        in_specs=[hbm] * 8,
         out_specs=(vmem, vmem, vmem),
         scratch_shapes=[
+            pltpu.SMEM(morton_pos.shape, I32),
+            pltpu.SMEM(neighbours.shape, I32),
+            pltpu.SMEM(rim.shape, I32),
+            pltpu.VMEM(features.shape, BF16),
+            pltpu.VMEM(cotangent.shape, BF16),
+            pltpu.VMEM(weight_one.shape, BF16),
+            pltpu.VMEM(weight_two.shape, BF16),
+            pltpu.VMEM((9 * PLANE, 9 * PLANE), BF16),
             pltpu.VMEM((2, 8, CH), I32),
             pltpu.SMEM((2, 8, CH), I32),
             pltpu.VMEM((2, 8, CH), I32),
@@ -481,23 +550,27 @@
             flat,
             pltpu.VMEM((2, 27 * CH, CH), F32),
             pltpu.VMEM((2, HALF, CH), F32),
-            pltpu.VMEM((2, n_x, QUARTER, CH), BF16),
-            pltpu.VMEM((2, n_x - 1, QUARTER, CH), BF16),
-            pltpu.VMEM((2, n_dev * 16, CH), F32),
-            pltpu.VMEM((2, n_dev, 16, CH), BF16),
-            pltpu.VMEM((2, n_dev - 1, 16, CH), BF16),
-            pltpu.VMEM((2, 2, n_x, n_dev, 16, CH), BF16),
+            pltpu.VMEM((2, 4, QUARTER, CH), BF16),
+            pltpu.VMEM((2, 3, QUARTER, CH), BF16),
+            pltpu.VMEM((2, 4, PIECE, CH), BF16),
+            pltpu.VMEM((2, 3, PIECE, CH), BF16),
+            pltpu.VMEM((2, 4 * PIECE, CH), F32),
+            pltpu.VMEM((2, 8, 16, CH), F32),
+            pltpu.VMEM((2, 7, 16, CH), F32),
+            pltpu.VMEM((2, 2, 4, 4, 8, 16, CH), BF16),
+            dma((8,)),
             dma((1,)),
             dma((2,)),
             dma((2,)),
             dma((2,)),
             dma((4, 4)),
             dma((4, 4)),
-            dma((2, 6)),
-            dma((2, 6)),
+            dma((2, 8)),
+            dma((2, 8)),
+            dma((2, 3)),
         ],
         compiler_params=pltpu.CompilerParams(
-            collective_id=0, has_side_effects=True, vmem_limit_bytes=48 * 1024 * 1024
+            collective_id=0, has_side_effects=True, vmem_limit_bytes=62 * 1024 * 1024
         ),
     )(
         morton_pos,
@@ -509,7 +582,7 @@
         weight_two,
         jnp.asarray(shift_matrix(), BF16),
     )
-    kernels = sums[:, :, :, :TILES].astype(F32).reshape(2, 27 * CH, CH)
+    kernels = sums.astype(F32).reshape(2, 27 * CH, CH)
     return (output, input_grad, kernels[0], kernels[1])
 
 

time: 129 us -> 118 us (0.915)
  local copies, waits for them, and re-layouts: 10.3 us -> 4.91 us
  Pallas kernels: 117 us -> 112 us
    unnamed x18 -> x6, local copies, waits for them, and re-layouts: 8.32 us -> 1.32 us
    pallas_call x1, Pallas kernels: 117 us -> 112 us  [per_device(): pl.pallas_call(functools.partial(unit_kernel, n_tile, n_dev, scale), out_...]
    slice x1, local copies, waits for them, and re-layouts: 2.02 us -> 3.59 us  [per_device(): return (output, input_grad, kernels[0], kernels[1])]
where the time goes in v2:
time: 118 us; the launch traced here: 117 us
  Pallas kernels  112 us (95%)
  local copies, waits for them, and re-layouts  4.91 us (4%)
    pallas_call x1, Pallas kernels, per_device(): pl.pallas_call(functools.partial(unit_kernel, n_tile, n_dev, scale), out_...  112 us
    slice x1, local copies, waits for them, and re-layouts, per_device(): return (output, input_grad, kernels[0], kernels[1])  3.59 us

profile of v2, /device:TPU:1, one launch (start us, length us, event | category | flops | bytes accessed | tf_op | source)
XLA Modules:
  0.0 117.5 jit_solution(4597255866973281684)
XLA Ops:
  0.6 111.9 %shard_map.111 = (bf16[8,64,128]{2,1,0:T(8,128)(2,1)}, bf16[8,64,128]{2,1,0:T(8,128)(2,1)}, bf16[2,2,4,27,16,128]{5,4,3,2,1,0:T(8,128)(2,1)}) custom-call(s32[8]{0:T(128)} %pos_in.1, s32[8,27]{1,0:T(8,128)} %nbr_in.1, s32[4]{0:T(128)} %rim_in.1, bf16[8,64,128]{2,1,0:T(8,128)(2,1)} %feat_in.1, bf16[8,64,128]{2,1,0:T(8,128)(2,1)} %cot_in.1, ...), custom_call_target="tpu_custom_call" | custom-call | tf_op jit(solution)/shard_map/pallas_call | solution.py:510
  112.6 0.0 copy-start.1
  112.6 0.0 copy-start
  112.6 3.6 %fusion = (f32[1,2,4,27,16,128]{5,4,3,2,1,0:T(8,128)}, f32[1,2,4,27,16,128]{5,4,3,2,1,0:T(8,128)}) fusion(bf16[2,2,4,27,16,128]{5,4,3,2,1,0:T(8,128)(2,1)} %get-tuple-element.9), kind=kLoop, calls=%fused_computation | loop fusion | bytes 7077888 | tf_op jit(solution)/shard_map/slice | solution.py:586
  116.2 0.0 copy-done.1
  116.2 0.7 copy.14
  116.8 0.0 copy-done
  116.8 0.7 copy.15
Async XLA Ops:
  112.6 3.6 %copy-start.1 = (bf16[8,64,128]{2,1,0:T(8,128)(2,1)S(1)}, bf16[8,64,128]{2,1,0:T(8,128)(2,1)}, u32[]{:S(2)}) copy-start(bf16[8,64,128]{2,1,0:T(8,128)(2,1)} %get-tuple-element.16) | copy-start | bytes 393220
  112.6 4.3 %copy-start = (bf16[8,64,128]{2,1,0:T(8,128)(2,1)S(1)}, bf16[8,64,128]{2,1,0:T(8,128)(2,1)}, u32[]{:S(2)}) copy-start(bf16[8,64,128]{2,1,0:T(8,128)(2,1)} %get-tuple-element.17) | copy-start | bytes 393220

commit v3 on v2

--- a/solution.py
+++ b/solution.py
@@ -162,7 +162,7 @@
     label_of_slot = jnp.min(jnp.where(hit, lax.rem(posv, BLK), BLK), axis=0, keepdims=True)
     idxv[0] = jnp.broadcast_to(row_of_slot, (8, CH))
     idxv[1] = jnp.minimum(slot_of_row, 2 * n_dev - 1)
-    labels[0] = jnp.broadcast_to(label_of_slot, (8, CH))
+    labels[0] = label_of_slot
     to_scalars = pltpu.make_async_copy(idxv, idxs, sem_local.at[0])
     to_scalars.start()
 
@@ -455,21 +455,24 @@
 
     returned[0] = repacked[0]
 
-    @pl.loop(1, n_dev)
-    def _(d):
-        where = lax.rem(dev - d + n_dev, n_dev)
-        remote(repacked.at[d], returned.at[d], sem_back.at[0], sem_back.at[1], dev=where).start()
-
-    for stage in (
-        start_second,
-        start_third,
-        start_gather_third,
-        start_gather_second,
-        start_gather_first,
-        start_gather_core,
+    order = [7 * i % n_dev for i in range(1, n_dev)]
+
+    def send_back(offsets):
+        for d in offsets:
+            where = lax.rem(dev - d + n_dev, n_dev)
+            remote(repacked.at[d], returned.at[d], sem_back.at[0], sem_back.at[1], dev=where).start()
+
+    for stage, offsets in (
+        (start_second, order[0:6]),
+        (start_third, order[6:12]),
+        (start_gather_third, order[12:18]),
+        (start_gather_second, order[18:24]),
+        (start_gather_first, order[24:]),
+        (start_gather_core, []),
     ):
         stage(1)
         stage(0)
+        send_back(offsets)
     await_bytes(returned.at[pl.ds(1, n_dev - 1)], sem_back.at[1])
     for r in range(BLK):
         linear = idxs[1, r, 0]
@@ -529,7 +532,7 @@
             pltpu.SMEM((2, 8, CH), I32),
             pltpu.VMEM((2, 8, CH), I32),
             pltpu.SMEM((2, 8, CH), I32),
-            pltpu.VMEM((n_dev, 8, CH), I32),
+            pltpu.VMEM((n_dev, 1, CH), I32),
             slab,
             slab,
             slab,

time: 118 us -> 103 us (0.87)
  Pallas kernels: 112 us -> 97.6 us
    pallas_call x1, Pallas kernels: 112 us -> 97.6 us  [per_device(): pl.pallas_call(functools.partial(unit_kernel, n_tile, n_dev, scale), out_...]
where the time goes in v3:
time: 103 us
  Pallas kernels  97.6 us (95%)
  local copies, waits for them, and re-layouts  4.91 us (5%)
    pallas_call x1, Pallas kernels, per_device(): pl.pallas_call(functools.partial(unit_kernel, n_tile, n_dev, scale), out_...  97.6 us
    slice x1, local copies, waits for them, and re-layouts, per_device(): return (output, input_grad, kernels[0], kernels[1])  3.59 us

profile of v3, /device:TPU:1, one launch (start us, length us, event | category | flops | bytes accessed | tf_op | source)
XLA Modules:
  0.0 103.2 jit_solution(6847373558995161522)
XLA Ops:
  0.6 97.6 %shard_map.111 = (bf16[8,64,128]{2,1,0:T(8,128)(2,1)}, bf16[8,64,128]{2,1,0:T(8,128)(2,1)}, bf16[2,2,4,27,16,128]{5,4,3,2,1,0:T(8,128)(2,1)}) custom-call(s32[8]{0:T(128)} %pos_in.1, s32[8,27]{1,0:T(8,128)} %nbr_in.1, s32[4]{0:T(128)} %rim_in.1, bf16[8,64,128]{2,1,0:T(8,128)(2,1)} %feat_in.1, bf16[8,64,128]{2,1,0:T(8,128)(2,1)} %cot_in.1, ...), custom_call_target="tpu_custom_call" | custom-call | tf_op jit(solution)/shard_map/pallas_call | solution.py:513
  98.2 0.0 copy-start.1
  98.2 0.0 copy-start
  98.3 3.6 %fusion = (f32[1,2,4,27,16,128]{5,4,3,2,1,0:T(8,128)}, f32[1,2,4,27,16,128]{5,4,3,2,1,0:T(8,128)}) fusion(bf16[2,2,4,27,16,128]{5,4,3,2,1,0:T(8,128)(2,1)} %get-tuple-element.9), kind=kLoop, calls=%fused_computation | loop fusion | bytes 7077888 | tf_op jit(solution)/shard_map/slice | solution.py:589
  101.8 0.0 copy-done.1
  101.8 0.7 copy.14
  102.5 0.0 copy-done
  102.5 0.7 copy.15
Async XLA Ops:
  98.2 3.6 %copy-start.1 = (bf16[8,64,128]{2,1,0:T(8,128)(2,1)S(1)}, bf16[8,64,128]{2,1,0:T(8,128)(2,1)}, u32[]{:S(2)}) copy-start(bf16[8,64,128]{2,1,0:T(8,128)(2,1)} %get-tuple-element.16) | copy-start | bytes 393220
  98.2 4.3 %copy-start = (bf16[8,64,128]{2,1,0:T(8,128)(2,1)S(1)}, bf16[8,64,128]{2,1,0:T(8,128)(2,1)}, u32[]{:S(2)}) copy-start(bf16[8,64,128]{2,1,0:T(8,128)(2,1)} %get-tuple-element.17) | copy-start | bytes 393220

commit v4 on v3

--- a/solution.py
+++ b/solution.py
@@ -78,6 +78,7 @@
     tab_h,
     tab_p,
     own,
+    leaving,
     rims,
     wt1,
     wt2,
@@ -107,6 +108,8 @@
     sem_sum_s,
     sem_sum_r,
     sem_first,
+    sem_core,
+    sem_out,
 ):
     tile = lax.axis_index("tile")
     dev = lax.axis_index("dev")
@@ -223,11 +226,15 @@
     def _(d):
         where = lax.rem(dev + d, n_dev)
         remote(labels.at[0], labels.at[d], sem_lab.at[0], sem_lab.at[1], dev=where).start()
-        remote(packed.at[d], arrived.at[d], sem_a2a.at[0], sem_a2a.at[1], dev=where).start()
 
     halo_c = halo_copies(0, tab_c)
     for copy in halo_c:
         copy.start()
+
+    @pl.loop(1, n_dev)
+    def _(d):
+        where = lax.rem(dev + d, n_dev)
+        remote(packed.at[d], arrived.at[d], sem_a2a.at[0], sem_a2a.at[1], dev=where).start()
 
     def flip_weights(source, target):
         for o in range(27):
@@ -235,17 +242,16 @@
             target[(26 - o) * CH : (27 - o) * CH, :] = piece.T.astype(BF16)
 
     def expand(table, y):
-        @pl.loop(0, BLK)
-        def _(b):
+        for b in range(BLK):
+            near = planes.at[b % 2]
             for i in range(6):
                 dx = 0 if i == 0 else (2 if i == 5 else 1)
                 row = (i + EDGE - 1) % EDGE
                 for t in range(9):
-                    entry = nbr[b, dx * 9 + t]
-                    planes[t * PLANE : (t + 1) * PLANE, i * CH : (i + 1) * CH] = table[
-                        entry, row * PLANE : (row + 1) * PLANE, :
+                    near[t * PLANE : (t + 1) * PLANE, i * CH : (i + 1) * CH] = table[
+                        nbr[b, dx * 9 + t], row * PLANE : (row + 1) * PLANE, :
                     ]
-            moved = dot(smat[...], planes[...]).astype(BF16)
+            moved = dot(smat[...], near[...]).astype(BF16)
             for i in range(6):
                 for t in range(9):
                     y[b, i, :, t * CH : (t + 1) * CH] = moved[
@@ -312,17 +318,25 @@
 
     partner = dict(tile=tile + 1 - 2 * core)
 
-    def half_rows(which):
-        return pl.ds(pl.multiple_of(which * HALF, 16), HALF)
-
-    def core_copy(q):
+    def core_copy(q, chunk):
+        start = pl.multiple_of((1 - core) * HALF + chunk * QUARTER, 16)
         return remote(
-            grads.at[q, half_rows(1 - core)],
-            core_in.at[q],
+            grads.at[q, pl.ds(start, QUARTER)],
+            core_in.at[q, chunk],
             sem_sum_s.at[q, 0],
-            sem_sum_r.at[q, 0],
+            sem_core.at[q, chunk],
             **partner,
         )
+
+    y = lax.rem(dev, 4)
+    z = dev // 4
+    n_z = n_dev // 4
+    dims = (("x", "y"), ("y", "x"))
+    place = dict(x=chip_x, y=y)
+
+    def start_core(q):
+        for e in (2, 1, 3, 0):
+            core_copy(q, lax.rem(place[dims[q][0]] + e, 4)).start()
 
     hidden_t = own[1].reshape(BLK * VOX, CH).astype(F32).T.astype(BF16)
     for kx in range(3):
@@ -330,18 +344,14 @@
         for t in range(9):
             o = 26 - (kx * 9 + t)
             grads[1, o * CH : (o + 1) * CH, :] = part[:, t * CH : (t + 1) * CH]
-    core_copy(1).start()
+    start_core(1)
     pre_grad_t = own[2].reshape(BLK * VOX, CH).astype(F32).T.astype(BF16)
     for kx in range(3):
         part = dot(pre_grad_t, columns(y_m, kx))
         for t in range(9):
             o = kx * 9 + t
             grads[0, o * CH : (o + 1) * CH, :] = part[:, t * CH : (t + 1) * CH].T
-    core_copy(0).start()
-
-    y = lax.rem(dev, 4)
-    z = dev // 4
-    n_z = n_dev // 4
+    start_core(0)
 
     def peer(dim, e):
         if dim == "x":
@@ -353,24 +363,20 @@
         other = lax.rem(z + e, n_z)
         return other, dict(dev=other * 4 + y)
 
-    dims = (("x", "y"), ("y", "x"))
-    place = dict(x=chip_x, y=y)
-
     def sem(q, stage):
         return sem_sum_s.at[q, stage], sem_sum_r.at[q, stage]
 
     def both_cores(q, chunk):
         start = pl.multiple_of(core * HALF + chunk * QUARTER, 16)
-        start_in = pl.multiple_of(chunk * QUARTER, 16)
-        return grads[q, pl.ds(start, QUARTER), :] + core_in[q, pl.ds(start_in, QUARTER), :]
+        return grads[q, pl.ds(start, QUARTER), :] + core_in[q, chunk]
 
     def start_first(q):
-        core_copy(q).wait_recv()
-        for j in range(4):
-            x_out[q, j] = both_cores(q, j).astype(BF16)
         for e in (2, 1, 3):
             other, where = peer(dims[q][0], e)
+            core_copy(q, other).wait_recv()
+            x_out[q, other] = both_cores(q, other).astype(BF16)
             remote(x_out.at[q, other], x_in.at[q, e - 1], *sem(q, 1), **where).start()
+        core_copy(q, place[dims[q][0]]).wait_recv()
 
     def start_second(q):
         await_bytes(x_in.at[q], sem_sum_r.at[q, 1])
@@ -419,6 +425,11 @@
         piece = final.at[q, core, chunk, :, pl.ds(0, 7)]
         return remote(piece, piece, *sem(q, 7), **partner)
 
+    def exit_copy(q, chunk):
+        return pltpu.make_async_copy(
+            final.at[q, core, chunk], out_sums.at[q, core, chunk], sem_out.at[q, chunk]
+        )
+
     def gather_first_copy(q, e):
         mine = final.at[q, core, place[dims[q][0]], :, pl.ds(0, 7)]
         _, where = peer(dims[q][0], e)
@@ -429,20 +440,25 @@
         for e in (2, 1, 3):
             gather_first_copy(q, e).start()
         gather_core_copy(q, place[dims[q][0]]).start()
+        exit_copy(q, place[dims[q][0]]).start()
 
     def start_gather_core(q):
         for e in (1, 3, 2):
+            chunk = lax.rem(place[dims[q][0]] + 4 - e, 4)
             gather_first_copy(q, e).wait_recv()
-            gather_core_copy(q, lax.rem(place[dims[q][0]] + 4 - e, 4)).start()
+            gather_core_copy(q, chunk).start()
+            exit_copy(q, chunk).start()
 
     start_first(1)
     start_first(0)
     finish_halo(halo_h, tab_h)
     expand(tab_h, y_x)
     pre_two = conv(y_x, w2)
-    out_output[...] = (
+    leaving[0] = (
         (own[0].reshape(BLK * VOX, CH).astype(F32) + pre_two).astype(BF16).reshape(BLK, VOX, CH)
     )
+    exit_output = pltpu.make_async_copy(leaving.at[0], out_output, sem_out.at[0, 5])
+    exit_output.start()
     finish_halo(halo_p, tab_p)
     expand(tab_p, y_x)
     back = conv(y_x, wt1) + cot[...].reshape(BLK * VOX, CH).astype(F32)
@@ -476,18 +492,20 @@
     await_bytes(returned.at[pl.ds(1, n_dev - 1)], sem_back.at[1])
     for r in range(BLK):
         linear = idxs[1, r, 0]
-        out_grad[r] = returned[linear // 2, lax.rem(linear, 2)]
+        leaving[1, r] = returned[linear // 2, lax.rem(linear, 2)]
+    exit_grad = pltpu.make_async_copy(leaving.at[1], out_grad, sem_out.at[1, 5])
+    exit_grad.start()
 
     await_bytes(labels.at[pl.ds(1, n_dev - 1)], sem_lab.at[0])
     await_bytes(packed.at[pl.ds(1, n_dev - 1)], sem_a2a.at[0])
     await_bytes(repacked.at[pl.ds(1, n_dev - 1)], sem_back.at[0])
+    for q in (1, 0):
+        await_bytes(final.at[q, 1 - core, :, :, pl.ds(0, 7)], sem_sum_r.at[q, 7])
+        pltpu.make_async_copy(
+            final.at[q, 1 - core], out_sums.at[q, 1 - core], sem_out.at[q, 4]
+        ).start()
     for q in range(2):
-        await_bytes(final.at[q, 1 - core, :, :, pl.ds(0, 7)], sem_sum_r.at[q, 7])
-        for c in range(2):
-            for j in range(4):
-                out_sums[q, c, j] = final[q, c, j, :, 0:7].reshape(28, 16, CH)[0:TILES]
-    for q in range(2):
-        core_copy(q).wait_send()
+        await_bytes(core_in.at[q], sem_sum_s.at[q, 0])
         await_bytes(x_in.at[q], sem_sum_s.at[q, 1])
         await_bytes(y_in.at[q], sem_sum_s.at[q, 2])
         await_bytes(z_in.at[q], sem_sum_s.at[q, 3])
@@ -495,6 +513,21 @@
         await_bytes(final.at[q, core, 0, pl.ds(0, 3), pl.ds(0, 7)], sem_sum_s.at[q, 5])
         await_bytes(final.at[q, core, pl.ds(0, 3), :, pl.ds(0, 7)], sem_sum_s.at[q, 6])
         await_bytes(final.at[q, core, :, :, pl.ds(0, 7)], sem_sum_s.at[q, 7])
+        for chunk in range(4):
+            exit_copy(q, chunk).wait()
+        pltpu.make_async_copy(
+            final.at[q, 1 - core], out_sums.at[q, 1 - core], sem_out.at[q, 4]
+        ).wait()
+    exit_output.wait()
+    exit_grad.wait()
+
+
+def finish_kernel(sums, output_in, grad_in, output, grad, grad_one, grad_two):
+    output[...] = output_in[...]
+    grad[...] = grad_in[...]
+    for q, target in enumerate((grad_one, grad_two)):
+        rows = sums[q, 0, 0, :, 0:7].reshape(4 * PIECE, CH)
+        target[...] = rows[0:QUARTER].astype(F32)
 
 
 def per_device(
@@ -504,7 +537,6 @@
     scale = 1.0 / math.sqrt(blocks * voxels * n_tile * n_dev)
     n_x = n_tile // 2
     hbm = pl.BlockSpec(memory_space=pltpu.HBM)
-    vmem = pl.BlockSpec(memory_space=pltpu.VMEM)
     dma = pltpu.SemaphoreType.DMA
     block_table = pltpu.VMEM((BLK + 4 * RIM + 1, VOX, CH), BF16)
     wide = pltpu.VMEM((BLK, 6, PLANE, 9 * CH), BF16)
@@ -515,10 +547,10 @@
         out_shape=(
             jax.ShapeDtypeStruct(features.shape, BF16),
             jax.ShapeDtypeStruct(features.shape, BF16),
-            jax.ShapeDtypeStruct((2, 2, 4, TILES, 16, CH), BF16),
+            jax.ShapeDtypeStruct((2, 2, 4, 4, 8, 16, CH), BF16),
         ),
         in_specs=[hbm] * 8,
-        out_specs=(vmem, vmem, vmem),
+        out_specs=(hbm, hbm, hbm),
         scratch_shapes=[
             pltpu.SMEM(morton_pos.shape, I32),
             pltpu.SMEM(neighbours.shape, I32),
@@ -542,17 +574,18 @@
             block_table,
             block_table,
             pltpu.VMEM((3, BLK, VOX, CH), BF16),
+            pltpu.VMEM((2, BLK, VOX, CH), BF16),
             pltpu.VMEM((4, RIM, VOX, CH), BF16),
             pltpu.VMEM((27 * CH, CH), BF16),
             pltpu.VMEM((27 * CH, CH), BF16),
-            pltpu.VMEM((9 * PLANE, 6 * CH), BF16),
+            pltpu.VMEM((2, 9 * PLANE, 6 * CH), BF16),
             wide,
             wide,
             wide,
             flat,
             flat,
             pltpu.VMEM((2, 27 * CH, CH), F32),
-            pltpu.VMEM((2, HALF, CH), F32),
+            pltpu.VMEM((2, 4, QUARTER, CH), F32),
             pltpu.VMEM((2, 4, QUARTER, CH), BF16),
             pltpu.VMEM((2, 3, QUARTER, CH), BF16),
             pltpu.VMEM((2, 4, PIECE, CH), BF16),
@@ -571,6 +604,8 @@
             dma((2, 8)),
             dma((2, 8)),
             dma((2, 3)),
+            dma((2, 4)),
+            dma((2, 6)),
         ],
         compiler_params=pltpu.CompilerParams(
             collective_id=0, has_side_effects=True, vmem_limit_bytes=62 * 1024 * 1024
@@ -585,8 +620,25 @@
         weight_two,
         jnp.asarray(shift_matrix(), BF16),
     )
-    kernels = sums.astype(F32).reshape(2, 27 * CH, CH)
-    return (output, input_grad, kernels[0], kernels[1])
+    one_block = pl.BlockSpec((1, voxels, channels), lambda i: (i, 0, 0))
+    kernel_rows = pl.BlockSpec((QUARTER, channels), lambda i: (i, 0))
+    kernel_shape = jax.ShapeDtypeStruct(weight_one.shape, F32)
+    return pl.pallas_call(
+        finish_kernel,
+        grid=(8,),
+        out_shape=(
+            jax.ShapeDtypeStruct(features.shape, BF16),
+            jax.ShapeDtypeStruct(features.shape, BF16),
+            kernel_shape,
+            kernel_shape,
+        ),
+        in_specs=[
+            pl.BlockSpec((2, 1, 1, 4, 8, 16, CH), lambda i: (0, i // 4, i % 4, 0, 0, 0, 0)),
+            one_block,
+            one_block,
+        ],
+        out_specs=(one_block, one_block, kernel_rows, kernel_rows),
+    )(sums, output, input_grad)
 
 
 def solution(mesh):

time: 103 us -> 97.2 us (0.944); the launches traced: 103 us -> 96.3 us
  local copies, waits for them, and re-layouts: 4.91 us -> 0 us
  Pallas kernels: 97.6 us -> 95.6 us
    pallas_call x1, Pallas kernels: 97.6 us -> 89.7 us  [per_device(): pl.pallas_call(functools.partial(unit_kernel, n_tile, n_dev, scale), out_...]
    pallas_call x0 -> x1, Pallas kernels: none -> 5.96 us  [per_device(): pl.pallas_call(finish_kernel, grid=(8,), out_shape=(jax.ShapeDtypeStruct(...]
    slice x1 -> x0, local copies, waits for them, and re-layouts: 3.59 us -> none  [per_device(): return (output, input_grad, kernels[0], kernels[1])]
    unnamed x6 -> x0, local copies, waits for them, and re-layouts: 1.32 us -> none
where the time goes in v4:
time: 97.2 us; the launch traced here: 96.3 us
  Pallas kernels  95.6 us (98%)
    pallas_call x1, Pallas kernels, per_device(): pl.pallas_call(functools.partial(unit_kernel, n_tile, n_dev, scale), out_...  89.7 us
    pallas_call x1, Pallas kernels, per_device(): pl.pallas_call(finish_kernel, grid=(8,), out_shape=(jax.ShapeDtypeStruct(...  5.96 us

profile of v4, /device:TPU:1, one launch (start us, length us, event | category | flops | bytes accessed | tf_op | source)
XLA Modules:
  0.0 96.3 jit_solution(6974759112991193802)
XLA Ops:
  0.6 89.7 %shard_map.111 = (bf16[8,64,128]{2,1,0:T(8,128)(2,1)}, bf16[8,64,128]{2,1,0:T(8,128)(2,1)}, bf16[2,2,4,4,8,16,128]{6,5,4,3,2,1,0:T(8,128)(2,1)}) custom-call(s32[8]{0:T(128)} %pos_in.1, s32[8,27]{1,0:T(8,128)} %nbr_in.1, s32[4]{0:T(128)} %rim_in.1, bf16[8,64,128]{2,1,0:T(8,128)(2,1)} %feat_in.1, bf16[8,64,128]{2,1,0:T(8,128)(2,1)} %cot_in.1, ...), custom_call_target="tpu_custom_call" | custom-call | tf_op jit(solution)/shard_map/pallas_call | solution.py:545
  90.3 6.0 %shard_map.112 = (bf16[8,64,128]{2,1,0:T(8,128)(2,1)}, bf16[8,64,128]{2,1,0:T(8,128)(2,1)}, f32[3456,128]{1,0:T(8,128)}, f32[3456,128]{1,0:T(8,128)}) custom-call(bf16[2,2,4,4,8,16,128]{6,5,4,3,2,1,0:T(8,128)(2,1)} %get-tuple-element.7.sums, bf16[8,64,128]{2,1,0:T(8,128)(2,1)} %get-tuple-element.8.output_in, bf16[8,64,128]{2,1,0:T(8,128)(2,1)} %get-tuple-element.9.grad_in), custom_call_target="tpu_custom_call" | custom-call | tf_op jit(solution)/shard_map/pallas_call | solution.py:626

commit v5 on v4

--- a/solution.py
+++ b/solution.py
@@ -522,12 +522,28 @@
     exit_grad.wait()
 
 
-def finish_kernel(sums, output_in, grad_in, output, grad, grad_one, grad_two):
-    output[...] = output_in[...]
-    grad[...] = grad_in[...]
-    for q, target in enumerate((grad_one, grad_two)):
-        rows = sums[q, 0, 0, :, 0:7].reshape(4 * PIECE, CH)
-        target[...] = rows[0:QUARTER].astype(F32)
+def finish_kernel(
+    sums, output_in, grad_in, output, grad, grad_one, grad_two, held, wide, sem_load, sem_store, sem_pass
+):
+    passes = [
+        pltpu.make_async_copy(output_in, output, sem_pass.at[0]),
+        pltpu.make_async_copy(grad_in, grad, sem_pass.at[1]),
+    ]
+    parts = [(q, c, j) for c in range(2) for j in range(4) for q in range(2)]
+    loads = [pltpu.make_async_copy(sums.at[part], held.at[part], sem_load.at[part]) for part in parts]
+    for copy in loads + passes:
+        copy.start()
+    stores = []
+    for part, load in zip(parts, loads):
+        q, c, j = part
+        load.wait()
+        rows = held[q, c, j, :, 0:7].reshape(4 * PIECE, CH)
+        wide[q, c, j] = rows[0:QUARTER].astype(F32)
+        target = (grad_one, grad_two)[q].at[pl.ds(c * HALF + j * QUARTER, QUARTER)]
+        stores.append(pltpu.make_async_copy(wide.at[part], target, sem_store.at[part]))
+        stores[-1].start()
+    for copy in stores + passes:
+        copy.wait()
 
 
 def per_device(
@@ -620,24 +636,25 @@
         weight_two,
         jnp.asarray(shift_matrix(), BF16),
     )
-    one_block = pl.BlockSpec((1, voxels, channels), lambda i: (i, 0, 0))
-    kernel_rows = pl.BlockSpec((QUARTER, channels), lambda i: (i, 0))
     kernel_shape = jax.ShapeDtypeStruct(weight_one.shape, F32)
     return pl.pallas_call(
         finish_kernel,
-        grid=(8,),
         out_shape=(
             jax.ShapeDtypeStruct(features.shape, BF16),
             jax.ShapeDtypeStruct(features.shape, BF16),
             kernel_shape,
             kernel_shape,
         ),
-        in_specs=[
-            pl.BlockSpec((2, 1, 1, 4, 8, 16, CH), lambda i: (0, i // 4, i % 4, 0, 0, 0, 0)),
-            one_block,
-            one_block,
+        in_specs=[hbm] * 3,
+        out_specs=(hbm,) * 4,
+        scratch_shapes=[
+            pltpu.VMEM((2, 2, 4, 4, 8, 16, CH), BF16),
+            pltpu.VMEM((2, 2, 4, QUARTER, CH), F32),
+            dma((2, 2, 4)),
+            dma((2, 2, 4)),
+            dma((2,)),
         ],
-        out_specs=(one_block, one_block, kernel_rows, kernel_rows),
+        compiler_params=pltpu.CompilerParams(vmem_limit_bytes=62 * 1024 * 1024),
     )(sums, output, input_grad)
 
 

time: 97.2 us -> 100 us (1.029)
  Pallas kernels: 95.6 us -> 98.9 us
    pallas_call x1, Pallas kernels: 5.96 us -> 9.37 us  [per_device(): pl.pallas_call(finish_kernel, out_shape=(jax.ShapeDtypeStruct(features.sh...]
where the time goes in v5:
time: 100 us; the launch traced here: 99.6 us
  Pallas kernels  98.9 us (99%)
    pallas_call x1, Pallas kernels, per_device(): pl.pallas_call(functools.partial(unit_kernel, n_tile, n_dev, scale), out_...  89.6 us
    pallas_call x1, Pallas kernels, per_device(): pl.pallas_call(finish_kernel, out_shape=(jax.ShapeDtypeStruct(features.sh...  9.37 us

profile of v5, /device:TPU:1, one launch (start us, length us, event | category | flops | bytes accessed | tf_op | source)
XLA Modules:
  0.0 99.6 jit_solution(12676470285975957149)
XLA Ops:
  0.6 89.6 %shard_map.111 = (bf16[8,64,128]{2,1,0:T(8,128)(2,1)}, bf16[8,64,128]{2,1,0:T(8,128)(2,1)}, bf16[2,2,4,4,8,16,128]{6,5,4,3,2,1,0:T(8,128)(2,1)}) custom-call(s32[8]{0:T(128)} %pos_in.1, s32[8,27]{1,0:T(8,128)} %nbr_in.1, s32[4]{0:T(128)} %rim_in.1, bf16[8,64,128]{2,1,0:T(8,128)(2,1)} %feat_in.1, bf16[8,64,128]{2,1,0:T(8,128)(2,1)} %cot_in.1, ...), custom_call_target="tpu_custom_call" | custom-call | tf_op jit(solution)/shard_map/pallas_call | solution.py:561
  90.2 9.4 %shard_map.112 = (bf16[8,64,128]{2,1,0:T(8,128)(2,1)}, bf16[8,64,128]{2,1,0:T(8,128)(2,1)}, f32[3456,128]{1,0:T(8,128)}, f32[3456,128]{1,0:T(8,128)}) custom-call(bf16[2,2,4,4,8,16,128]{6,5,4,3,2,1,0:T(8,128)(2,1)} %get-tuple-element.7.sums, bf16[8,64,128]{2,1,0:T(8,128)(2,1)} %get-tuple-element.8.output_in, bf16[8,64,128]{2,1,0:T(8,128)(2,1)} %get-tuple-element.9.grad_in), custom_call_target="tpu_custom_call" | custom-call | tf_op jit(solution)/shard_map/pallas_call | solution.py:640

commit v6 on v5

--- a/solution.py
+++ b/solution.py
@@ -69,8 +69,15 @@
     slotv,
     slots,
     labels,
-    packed,
-    arrived,
+    z_labels,
+    z_slotv,
+    z_slots,
+    ring_0,
+    ring_1,
+    ring_2,
+    ring_3,
+    y_send,
+    y_got,
     repacked,
     returned,
     tab_m,
@@ -100,7 +107,10 @@
     final,
     sem_in,
     sem_local,
-    sem_a2a,
+    sem_ring_s,
+    sem_ring_r,
+    sem_y,
+    sem_z_lab,
     sem_lab,
     sem_back,
     sem_halo_s,
@@ -213,28 +223,61 @@
     load_feat.wait()
     to_scalars.wait()
 
-    @pl.loop(0, n_dev)
-    def _(d):
-        for c in range(2):
-            packed[d, c] = feat[idxs[0, 0, 2 * d + c]]
-
-    arrived[0] = packed[0]
+    rings = (ring_0, ring_1, ring_2, ring_3)
+    for p, ring in enumerate(rings):
+        ring[0:BLK] = feat[:, p * PLANE : (p + 1) * PLANE, :]
+        ring[8 * BLK] = jnp.zeros((PLANE, CH), BF16)
+    pos_lanes = jnp.zeros((1, CH), I32)
+    for r in range(BLK):
+        pos_lanes = jnp.where(lax.rem(lane[0:1], BLK) == r, pos[r], pos_lanes)
+    z_labels[0] = pos_lanes
+
+    y = lax.rem(dev, 4)
+    z = dev // 4
+    n_z = n_dev // 4
+
+    def ring_copy(step, p, ahead):
+        source = step - 1 if ahead else (9 - step) % 8
+        target = step if ahead else 8 - step
+        where = lax.rem(dev + (4 if ahead else n_dev - 4), n_dev)
+        return remote(
+            rings[p].at[pl.ds(source * BLK, BLK)],
+            rings[p].at[pl.ds(target * BLK, BLK)],
+            sem_ring_s.at[p],
+            sem_ring_r.at[target, p],
+            dev=where,
+        )
+
+    def ring_starts(step, p):
+        if step < 4:
+            return [ring_copy(step, p, True), ring_copy(step, p, False)]
+        return [ring_copy(4, p, p < 2)]
+
+    def ring_step(step):
+        for p in range(4):
+            arriving = ring_starts(step, p)
+            leaving_now = ring_starts(step + 1, p)
+            for copy in arriving:
+                copy.wait_recv()
+            for copy in leaving_now:
+                copy.start()
 
     pl.semaphore_wait(barrier, n_dev + n_tile - 2)
+
+    for k in range(1, n_z):
+        where = lax.rem(dev + 4 * k, n_dev)
+        remote(z_labels.at[0], z_labels.at[k], sem_z_lab.at[0], sem_z_lab.at[1], dev=where).start()
+    for p in range(4):
+        for copy in ring_starts(1, p):
+            copy.start()
+    halo_c = halo_copies(0, tab_c)
+    for copy in halo_c:
+        copy.start()
 
     @pl.loop(1, n_dev)
     def _(d):
         where = lax.rem(dev + d, n_dev)
         remote(labels.at[0], labels.at[d], sem_lab.at[0], sem_lab.at[1], dev=where).start()
-
-    halo_c = halo_copies(0, tab_c)
-    for copy in halo_c:
-        copy.start()
-
-    @pl.loop(1, n_dev)
-    def _(d):
-        where = lax.rem(dev + d, n_dev)
-        remote(packed.at[d], arrived.at[d], sem_a2a.at[0], sem_a2a.at[1], dev=where).start()
 
     def flip_weights(source, target):
         for o in range(27):
@@ -274,31 +317,55 @@
     flip_weights(w1, wt1)
     load_smat.wait()
     load_nbr.wait()
+    ring_step(1)
     finish_halo(halo_c, tab_c)
     expand(tab_c, y_c)
+    ring_step(2)
     hidden_grad[...] = conv(y_c, wt2)
-
-    await_bytes(labels.at[pl.ds(1, n_dev - 1)], sem_lab.at[1])
-    label_at = jnp.zeros((8, CH), I32)
-    for d in range(n_dev):
-        label_at = jnp.where(lane // 2 == d, labels[d], label_at)
-    label_at = jnp.where(lane < 2 * n_dev, label_at, BLK)
-    slotv[0] = jnp.minimum(label_at, BLK - 1)
-    slotv[1] = jnp.broadcast_to(
-        jnp.max(jnp.where(label_at == sub, lane, 0), axis=1, keepdims=True), (8, CH)
-    )
-    to_slots = pltpu.make_async_copy(slotv, slots, sem_local.at[0])
-    to_slots.start()
-    to_slots.wait()
-    await_bytes(arrived.at[pl.ds(1, n_dev - 1)], sem_a2a.at[1])
-    for s in range(BLK):
-        linear = slots[1, s, 0]
-        own[0, s] = arrived[linear // 2, lax.rem(linear, 2)]
+    await_bytes(z_labels.at[pl.ds(1, n_z - 1)], sem_z_lab.at[1])
+    z_pos = jnp.full((8, CH), -1, I32)
+    for k in range(n_z):
+        z_pos = jnp.where(lane // BLK == k, z_labels[k], z_pos)
+    for dy in range(4):
+        wanted = (z * 4 + lax.rem(y + dy, 4)) * BLK + sub
+        found = jnp.min(jnp.where(z_pos == wanted, lane, 8 * BLK), axis=1, keepdims=True)
+        z_slotv[dy] = jnp.broadcast_to(found, (8, CH))
+    to_z_slots = pltpu.make_async_copy(z_slotv, z_slots, sem_local.at[0])
+    to_z_slots.start()
+    to_z_slots.wait()
+    ring_step(3)
+
+    def y_copy(p, dy):
+        where = dict(dev=z * 4 + lax.rem(y + dy, 4))
+        return remote(y_send.at[p, dy], y_got.at[p, dy - 1], sem_y.at[0, p], sem_y.at[1, p], **where)
+
+    for p in (0, 2, 1, 3):
+        for copy in ring_starts(4, p):
+            copy.wait_recv()
+        for dy in (2, 1, 3, 0):
+            for s in range(BLK):
+                y_send[p, dy, s] = rings[p][z_slots[dy, s, 0]]
+            if dy:
+                y_copy(p, dy).start()
+    for p in (0, 2, 1, 3):
+        await_bytes(y_got.at[p], sem_y.at[1, p])
+        rows = y_send[p, 0].astype(F32)
+        for dy in range(3):
+            rows = rows + y_got[p, dy].astype(F32)
+        own[0, :, p * PLANE : (p + 1) * PLANE, :] = rows.astype(BF16)
     tab_m[0:BLK] = own[0]
     pack_rims(own.at[0], 1)
     halo_m = halo_copies(1, tab_m)
     for copy in halo_m:
         copy.start()
+    await_bytes(labels.at[pl.ds(1, n_dev - 1)], sem_lab.at[1])
+    label_at = jnp.zeros((8, CH), I32)
+    for d in range(n_dev):
+        label_at = jnp.where(lane // 2 == d, labels[d], label_at)
+    slotv[0] = jnp.minimum(label_at, BLK - 1)
+    to_slots = pltpu.make_async_copy(slotv, slots, sem_local.at[0])
+    to_slots.start()
+    to_slots.wait()
     finish_halo(halo_m, tab_m)
     expand(tab_m, y_m)
     pre = conv(y_m, w1)
@@ -328,9 +395,6 @@
             **partner,
         )
 
-    y = lax.rem(dev, 4)
-    z = dev // 4
-    n_z = n_dev // 4
     dims = (("x", "y"), ("y", "x"))
     place = dict(x=chip_x, y=y)
 
@@ -497,7 +561,10 @@
     exit_grad.start()
 
     await_bytes(labels.at[pl.ds(1, n_dev - 1)], sem_lab.at[0])
-    await_bytes(packed.at[pl.ds(1, n_dev - 1)], sem_a2a.at[0])
+    await_bytes(z_labels.at[pl.ds(1, n_z - 1)], sem_z_lab.at[0])
+    for p in range(4):
+        await_bytes(rings[p].at[pl.ds(0, 7 * BLK)], sem_ring_s.at[p])
+        await_bytes(y_got.at[p], sem_y.at[0, p])
     await_bytes(repacked.at[pl.ds(1, n_dev - 1)], sem_back.at[0])
     for q in (1, 0):
         await_bytes(final.at[q, 1 - core, :, :, pl.ds(0, 7)], sem_sum_r.at[q, 7])
@@ -523,17 +590,23 @@
 
 
 def finish_kernel(
-    sums, output_in, grad_in, output, grad, grad_one, grad_two, held, wide, sem_load, sem_store, sem_pass
+    sums, output_in, grad_in, output, grad, grad_one, grad_two, rows_held, held, wide, sem_load, sem_store, sem_pass
 ):
     passes = [
-        pltpu.make_async_copy(output_in, output, sem_pass.at[0]),
-        pltpu.make_async_copy(grad_in, grad, sem_pass.at[1]),
+        pltpu.make_async_copy(output_in, rows_held.at[0], sem_pass.at[0]),
+        pltpu.make_async_copy(grad_in, rows_held.at[1], sem_pass.at[1]),
     ]
     parts = [(q, c, j) for c in range(2) for j in range(4) for q in range(2)]
     loads = [pltpu.make_async_copy(sums.at[part], held.at[part], sem_load.at[part]) for part in parts]
-    for copy in loads + passes:
+    for copy in passes + loads:
         copy.start()
-    stores = []
+    stores = [
+        pltpu.make_async_copy(rows_held.at[0], output, sem_pass.at[2]),
+        pltpu.make_async_copy(rows_held.at[1], grad, sem_pass.at[3]),
+    ]
+    for copy, store in zip(passes, stores):
+        copy.wait()
+        store.start()
     for part, load in zip(parts, loads):
         q, c, j = part
         load.wait()
@@ -542,7 +615,7 @@
         target = (grad_one, grad_two)[q].at[pl.ds(c * HALF + j * QUARTER, QUARTER)]
         stores.append(pltpu.make_async_copy(wide.at[part], target, sem_store.at[part]))
         stores[-1].start()
-    for copy in stores + passes:
+    for copy in stores:
         copy.wait()
 
 
@@ -557,6 +630,7 @@
     block_table = pltpu.VMEM((BLK + 4 * RIM + 1, VOX, CH), BF16)
     wide = pltpu.VMEM((BLK, 6, PLANE, 9 * CH), BF16)
     flat = pltpu.VMEM((BLK * VOX, CH), F32)
+    ring = pltpu.VMEM((9 * BLK, PLANE, CH), BF16)
     slab = pltpu.VMEM((n_dev, 2, VOX, CH), BF16)
     output, input_grad, sums = pl.pallas_call(
         functools.partial(unit_kernel, n_tile, n_dev, scale),
@@ -581,8 +655,15 @@
             pltpu.VMEM((2, 8, CH), I32),
             pltpu.SMEM((2, 8, CH), I32),
             pltpu.VMEM((n_dev, 1, CH), I32),
-            slab,
-            slab,
+            pltpu.VMEM((8, 1, CH), I32),
+            pltpu.VMEM((4, 8, CH), I32),
+            pltpu.SMEM((4, 8, CH), I32),
+            ring,
+            ring,
+            ring,
+            ring,
+            pltpu.VMEM((4, 4, BLK, PLANE, CH), BF16),
+            pltpu.VMEM((4, 3, BLK, PLANE, CH), BF16),
             slab,
             slab,
             block_table,
@@ -612,6 +693,9 @@
             pltpu.VMEM((2, 2, 4, 4, 8, 16, CH), BF16),
             dma((8,)),
             dma((1,)),
+            dma((4,)),
+            dma((8, 4)),
+            dma((2, 4)),
             dma((2,)),
             dma((2,)),
             dma((2,)),
@@ -648,11 +732,12 @@
         in_specs=[hbm] * 3,
         out_specs=(hbm,) * 4,
         scratch_shapes=[
+            pltpu.VMEM((2,) + features.shape, BF16),
             pltpu.VMEM((2, 2, 4, 4, 8, 16, CH), BF16),
             pltpu.VMEM((2, 2, 4, QUARTER, CH), F32),
             dma((2, 2, 4)),
             dma((2, 2, 4)),
-            dma((2,)),
+            dma((4,)),
         ],
         compiler_params=pltpu.CompilerParams(vmem_limit_bytes=62 * 1024 * 1024),
     )(sums, output, input_grad)

time: 100 us -> 90.4 us (0.904)
  Pallas kernels: 98.9 us -> 88.7 us
    pallas_call x1, Pallas kernels: 9.37 us -> 3.77 us  [per_device(): pl.pallas_call(finish_kernel, out_shape=(jax.ShapeDtypeStruct(features.sh...]
    pallas_call x1, Pallas kernels: 89.6 us -> 85 us  [per_device(): pl.pallas_call(functools.partial(unit_kernel, n_tile, n_dev, scale), out_...]
where the time goes in v6:
time: 90.4 us; the launch traced here: 89.5 us
  Pallas kernels  88.7 us (98%)
    pallas_call x1, Pallas kernels, per_device(): pl.pallas_call(functools.partial(unit_kernel, n_tile, n_dev, scale), out_...  85 us
    pallas_call x1, Pallas kernels, per_device(): pl.pallas_call(finish_kernel, out_shape=(jax.ShapeDtypeStruct(features.sh...  3.77 us

profile of v6, /device:TPU:1, one launch (start us, length us, event | category | flops | bytes accessed | tf_op | source)
XLA Modules:
  0.0 89.5 jit_solution(10347758418190513919)
XLA Ops:
  0.6 85.0 %shard_map.111 = (bf16[8,64,128]{2,1,0:T(8,128)(2,1)}, bf16[8,64,128]{2,1,0:T(8,128)(2,1)}, bf16[2,2,4,4,8,16,128]{6,5,4,3,2,1,0:T(8,128)(2,1)}) custom-call(s32[8]{0:T(128)} %pos_in.1, s32[8,27]{1,0:T(8,128)} %nbr_in.1, s32[4]{0:T(128)} %rim_in.1, bf16[8,64,128]{2,1,0:T(8,128)(2,1)} %feat_in.1, bf16[8,64,128]{2,1,0:T(8,128)(2,1)} %cot_in.1, ...), custom_call_target="tpu_custom_call" | custom-call | tf_op jit(solution)/shard_map/pallas_call | solution.py:635
  85.6 3.8 %shard_map.112 = (bf16[8,64,128]{2,1,0:T(8,128)(2,1)}, bf16[8,64,128]{2,1,0:T(8,128)(2,1)}, f32[3456,128]{1,0:T(8,128)}, f32[3456,128]{1,0:T(8,128)}) custom-call(bf16[2,2,4,4,8,16,128]{6,5,4,3,2,1,0:T(8,128)(2,1)} %get-tuple-element.7.sums, bf16[8,64,128]{2,1,0:T(8,128)(2,1)} %get-tuple-element.8.output_in, bf16[8,64,128]{2,1,0:T(8,128)(2,1)} %get-tuple-element.9.grad_in), custom_call_target="tpu_custom_call" | custom-call | tf_op jit(solution)/shard_map/pallas_call | solution.py:724

commit v7 on v6

--- a/solution.py
+++ b/solution.py
@@ -149,6 +149,8 @@
     load_pos, load_rim, load_feat, load_cot, load_w2, load_w1, load_smat, load_nbr = loads
     for load in loads:
         load.start()
+    for table in (tab_m, tab_c, tab_h, tab_p):
+        table[BLK + 2 * RIM :] = jnp.zeros((2 * RIM + 1, EDGE, PLANE, CH), BF16)
     barrier = pltpu.get_barrier_semaphore()
 
     @pl.loop(1, n_dev)
@@ -181,22 +183,23 @@
 
     def pack_rims(rows, which):
         for h in range(RIM):
-            rims[which, h] = rows[rim[h]]
+            rims[which, h] = rows[rim[h]].reshape(EDGE, PLANE, CH)
 
     def halo_copies(which, table):
         result = []
-        for q, where in enumerate(
+        every, low, high = slice(None), pl.ds(0, PLANE // 2), pl.ds(PLANE // 2, PLANE // 2)
+        for q, (where, part) in enumerate(
             (
-                dict(tile=lax.rem(tile + 1, n_tile)),
-                dict(tile=lax.rem(tile + n_tile - 1, n_tile)),
-                dict(dev=lax.rem(dev + 1, n_dev)),
-                dict(dev=lax.rem(dev + n_dev - 1, n_dev)),
+                (dict(tile=lax.rem(tile + 1, n_tile)), (pl.ds(EDGE - 1, 1), every)),
+                (dict(tile=lax.rem(tile + n_tile - 1, n_tile)), (pl.ds(0, 1), every)),
+                (dict(dev=lax.rem(dev + 1, n_dev)), (every, high)),
+                (dict(dev=lax.rem(dev + n_dev - 1, n_dev)), (every, low)),
             )
         ):
             result.append(
                 remote(
-                    rims.at[which],
-                    table.at[pl.ds(BLK + q * RIM, RIM)],
+                    rims.at[(which, every) + part],
+                    table.at[(pl.ds(BLK + q * RIM, RIM),) + part],
                     sem_halo_s.at[which, q],
                     sem_halo_r.at[which, q],
                     **where,
@@ -212,13 +215,11 @@
 
             @pl.when(edge)
             def _(q=q):
-                table[BLK + q * RIM : BLK + (q + 1) * RIM] = jnp.zeros((RIM, VOX, CH), BF16)
-
-    for table in (tab_m, tab_c, tab_h, tab_p):
-        table[BLK + 4 * RIM] = jnp.zeros((VOX, CH), BF16)
+                table[BLK + q * RIM : BLK + (q + 1) * RIM] = jnp.zeros((RIM, EDGE, PLANE, CH), BF16)
+
     load_rim.wait()
     load_cot.wait()
-    tab_c[0:BLK] = cot[...]
+    tab_c[0:BLK] = cot[...].reshape(BLK, EDGE, PLANE, CH)
     pack_rims(cot, 0)
     load_feat.wait()
     to_scalars.wait()
@@ -292,7 +293,7 @@
                 row = (i + EDGE - 1) % EDGE
                 for t in range(9):
                     near[t * PLANE : (t + 1) * PLANE, i * CH : (i + 1) * CH] = table[
-                        nbr[b, dx * 9 + t], row * PLANE : (row + 1) * PLANE, :
+                        nbr[b, dx * 9 + t], row
                     ]
             moved = dot(smat[...], near[...]).astype(BF16)
             for i in range(6):
@@ -353,7 +354,7 @@
         for dy in range(3):
             rows = rows + y_got[p, dy].astype(F32)
         own[0, :, p * PLANE : (p + 1) * PLANE, :] = rows.astype(BF16)
-    tab_m[0:BLK] = own[0]
+    tab_m[0:BLK] = own[0].reshape(BLK, EDGE, PLANE, CH)
     pack_rims(own.at[0], 1)
     halo_m = halo_copies(1, tab_m)
     for copy in halo_m:
@@ -372,8 +373,8 @@
     gate = jax.nn.sigmoid(pre)
     hidden = (pre * gate).astype(BF16)
     pre_grad = (hidden_grad[...] * gate * (1.0 + pre * (1.0 - gate))).astype(BF16)
-    tab_h[0:BLK] = hidden.reshape(BLK, VOX, CH)
-    tab_p[0:BLK] = pre_grad.reshape(BLK, VOX, CH)
+    tab_h[0:BLK] = hidden.reshape(BLK, EDGE, PLANE, CH)
+    tab_p[0:BLK] = pre_grad.reshape(BLK, EDGE, PLANE, CH)
     own[1] = hidden.reshape(BLK, VOX, CH)
     own[2] = pre_grad.reshape(BLK, VOX, CH)
     pack_rims(own.at[1], 2)
@@ -627,7 +628,7 @@
     n_x = n_tile // 2
     hbm = pl.BlockSpec(memory_space=pltpu.HBM)
     dma = pltpu.SemaphoreType.DMA
-    block_table = pltpu.VMEM((BLK + 4 * RIM + 1, VOX, CH), BF16)
+    block_table = pltpu.VMEM((BLK + 4 * RIM + 1, EDGE, PLANE, CH), BF16)
     wide = pltpu.VMEM((BLK, 6, PLANE, 9 * CH), BF16)
     flat = pltpu.VMEM((BLK * VOX, CH), F32)
     ring = pltpu.VMEM((9 * BLK, PLANE, CH), BF16)
@@ -672,7 +673,7 @@
             block_table,
             pltpu.VMEM((3, BLK, VOX, CH), BF16),
             pltpu.VMEM((2, BLK, VOX, CH), BF16),
-            pltpu.VMEM((4, RIM, VOX, CH), BF16),
+            pltpu.VMEM((4, RIM, EDGE, PLANE, CH), BF16),
             pltpu.VMEM((27 * CH, CH), BF16),
             pltpu.VMEM((27 * CH, CH), BF16),
             pltpu.VMEM((2, 9 * PLANE, 6 * CH), BF16),

time: 90.4 us -> 89.2 us (0.987)
  no operation moved by 1% of the time
where the time goes in v7:
time: 89.2 us; the launch traced here: 88.9 us
  Pallas kernels  88.1 us (99%)
    pallas_call x1, Pallas kernels, per_device(): pl.pallas_call(functools.partial(unit_kernel, n_tile, n_dev, scale), out_...  84.3 us
    pallas_call x1, Pallas kernels, per_device(): pl.pallas_call(finish_kernel, out_shape=(jax.ShapeDtypeStruct(features.sh...  3.77 us

profile of v7, /device:TPU:1, one launch (start us, length us, event | category | flops | bytes accessed | tf_op | source)
XLA Modules:
  0.0 88.9 jit_solution(9814992420542197914)
XLA Ops:
  0.6 84.3 %shard_map.111 = (bf16[8,64,128]{2,1,0:T(8,128)(2,1)}, bf16[8,64,128]{2,1,0:T(8,128)(2,1)}, bf16[2,2,4,4,8,16,128]{6,5,4,3,2,1,0:T(8,128)(2,1)}) custom-call(s32[8]{0:T(128)} %pos_in.1, s32[8,27]{1,0:T(8,128)} %nbr_in.1, s32[4]{0:T(128)} %rim_in.1, bf16[8,64,128]{2,1,0:T(8,128)(2,1)} %feat_in.1, bf16[8,64,128]{2,1,0:T(8,128)(2,1)} %cot_in.1, ...), custom_call_target="tpu_custom_call" | custom-call | tf_op jit(solution)/shard_map/pallas_call | solution.py:636
  85.0 3.8 %shard_map.112 = (bf16[8,64,128]{2,1,0:T(8,128)(2,1)}, bf16[8,64,128]{2,1,0:T(8,128)(2,1)}, f32[3456,128]{1,0:T(8,128)}, f32[3456,128]{1,0:T(8,128)}) custom-call(bf16[2,2,4,4,8,16,128]{6,5,4,3,2,1,0:T(8,128)(2,1)} %get-tuple-element.7.sums, bf16[8,64,128]{2,1,0:T(8,128)(2,1)} %get-tuple-element.8.output_in, bf16[8,64,128]{2,1,0:T(8,128)(2,1)} %get-tuple-element.9.grad_in), custom_call_target="tpu_custom_call" | custom-call | tf_op jit(solution)/shard_map/pallas_call | solution.py:725

commit v8 on v7

--- a/solution.py
+++ b/solution.py
@@ -543,11 +543,12 @@
             where = lax.rem(dev - d + n_dev, n_dev)
             remote(repacked.at[d], returned.at[d], sem_back.at[0], sem_back.at[1], dev=where).start()
 
+    send_back(order[0:4])
     for stage, offsets in (
-        (start_second, order[0:6]),
-        (start_third, order[6:12]),
-        (start_gather_third, order[12:18]),
-        (start_gather_second, order[18:24]),
+        (start_second, order[4:9]),
+        (start_third, order[9:14]),
+        (start_gather_third, order[14:19]),
+        (start_gather_second, order[19:24]),
         (start_gather_first, order[24:]),
         (start_gather_core, []),
     ):

time: 89.2 us -> 90 us (level)
  the two profiles are of different devices: /device:TPU:1 before, /device:TPU:9 now
where the time goes in v8:
time: 90 us; the launch traced here: 89.9 us
  Pallas kernels  89.1 us (99%)
    pallas_call x1, Pallas kernels, per_device(): pl.pallas_call(functools.partial(unit_kernel, n_tile, n_dev, scale), out_...  85.3 us
    pallas_call x1, Pallas kernels, per_device(): pl.pallas_call(finish_kernel, out_shape=(jax.ShapeDtypeStruct(features.sh...  3.77 us

profile of v8, /device:TPU:9, one launch (start us, length us, event | category | flops | bytes accessed | tf_op | source)
XLA Modules:
  0.0 89.9 jit_solution(15634864185837704947)
XLA Ops:
  0.6 85.3 %shard_map.111 = (bf16[8,64,128]{2,1,0:T(8,128)(2,1)}, bf16[8,64,128]{2,1,0:T(8,128)(2,1)}, bf16[2,2,4,4,8,16,128]{6,5,4,3,2,1,0:T(8,128)(2,1)}) custom-call(s32[8]{0:T(128)} %pos_in.1, s32[8,27]{1,0:T(8,128)} %nbr_in.1, s32[4]{0:T(128)} %rim_in.1, bf16[8,64,128]{2,1,0:T(8,128)(2,1)} %feat_in.1, bf16[8,64,128]{2,1,0:T(8,128)(2,1)} %cot_in.1, ...), custom_call_target="tpu_custom_call" | custom-call | tf_op jit(solution)/shard_map/pallas_call | solution.py:637
  85.9 3.8 %shard_map.112 = (bf16[8,64,128]{2,1,0:T(8,128)(2,1)}, bf16[8,64,128]{2,1,0:T(8,128)(2,1)}, f32[3456,128]{1,0:T(8,128)}, f32[3456,128]{1,0:T(8,128)}) custom-call(bf16[2,2,4,4,8,16,128]{6,5,4,3,2,1,0:T(8,128)(2,1)} %get-tuple-element.7.sums, bf16[8,64,128]{2,1,0:T(8,128)(2,1)} %get-tuple-element.8.output_in, bf16[8,64,128]{2,1,0:T(8,128)(2,1)} %get-tuple-element.9.grad_in), custom_call_target="tpu_custom_call" | custom-call | tf_op jit(solution)/shard_map/pallas_call | solution.py:726

commit v9 on v7

--- a/solution.py
+++ b/solution.py
@@ -544,11 +544,11 @@
             remote(repacked.at[d], returned.at[d], sem_back.at[0], sem_back.at[1], dev=where).start()
 
     for stage, offsets in (
-        (start_second, order[0:6]),
-        (start_third, order[6:12]),
-        (start_gather_third, order[12:18]),
-        (start_gather_second, order[18:24]),
-        (start_gather_first, order[24:]),
+        (start_second, order[0:5]),
+        (start_third, order[5:8]),
+        (start_gather_third, order[8:12]),
+        (start_gather_second, order[12:20]),
+        (start_gather_first, order[20:]),
         (start_gather_core, []),
     ):
         stage(1)

time: 89.2 us -> 89.2 us (level); the launches traced: 88.9 us -> 87.4 us
  Pallas kernels: 88.1 us -> 86.6 us
    pallas_call x1, Pallas kernels: 84.3 us -> 82.9 us  [per_device(): pl.pallas_call(functools.partial(unit_kernel, n_tile, n_dev, scale), out_...]
where the time goes in v9:
time: 89.2 us; the launch traced here: 87.4 us
  Pallas kernels  86.6 us (97%)
    pallas_call x1, Pallas kernels, per_device(): pl.pallas_call(functools.partial(unit_kernel, n_tile, n_dev, scale), out_...  82.9 us
    pallas_call x1, Pallas kernels, per_device(): pl.pallas_call(finish_kernel, out_shape=(jax.ShapeDtypeStruct(features.sh...  3.77 us

profile of v9, /device:TPU:1, one launch (start us, length us, event | category | flops | bytes accessed | tf_op | source)
XLA Modules:
  0.0 87.4 jit_solution(238304891968896090)
XLA Ops:
  0.6 82.9 %shard_map.111 = (bf16[8,64,128]{2,1,0:T(8,128)(2,1)}, bf16[8,64,128]{2,1,0:T(8,128)(2,1)}, bf16[2,2,4,4,8,16,128]{6,5,4,3,2,1,0:T(8,128)(2,1)}) custom-call(s32[8]{0:T(128)} %pos_in.1, s32[8,27]{1,0:T(8,128)} %nbr_in.1, s32[4]{0:T(128)} %rim_in.1, bf16[8,64,128]{2,1,0:T(8,128)(2,1)} %feat_in.1, bf16[8,64,128]{2,1,0:T(8,128)(2,1)} %cot_in.1, ...), custom_call_target="tpu_custom_call" | custom-call | tf_op jit(solution)/shard_map/pallas_call | solution.py:636
  83.5 3.8 %shard_map.112 = (bf16[8,64,128]{2,1,0:T(8,128)(2,1)}, bf16[8,64,128]{2,1,0:T(8,128)(2,1)}, f32[3456,128]{1,0:T(8,128)}, f32[3456,128]{1,0:T(8,128)}) custom-call(bf16[2,2,4,4,8,16,128]{6,5,4,3,2,1,0:T(8,128)(2,1)} %get-tuple-element.7.sums, bf16[8,64,128]{2,1,0:T(8,128)(2,1)} %get-tuple-element.8.output_in, bf16[8,64,128]{2,1,0:T(8,128)(2,1)} %get-tuple-element.9.grad_in), custom_call_target="tpu_custom_call" | custom-call | tf_op jit(solution)/shard_map/pallas_call | solution.py:725

commit v10 on v7

--- a/solution.py
+++ b/solution.py
@@ -377,12 +377,6 @@
     tab_p[0:BLK] = pre_grad.reshape(BLK, EDGE, PLANE, CH)
     own[1] = hidden.reshape(BLK, VOX, CH)
     own[2] = pre_grad.reshape(BLK, VOX, CH)
-    pack_rims(own.at[1], 2)
-    pack_rims(own.at[2], 3)
-    halo_h = halo_copies(2, tab_h)
-    halo_p = halo_copies(3, tab_p)
-    for copy in halo_h + halo_p:
-        copy.start()
 
     partner = dict(tile=tile + 1 - 2 * core)
 
@@ -410,6 +404,12 @@
             o = 26 - (kx * 9 + t)
             grads[1, o * CH : (o + 1) * CH, :] = part[:, t * CH : (t + 1) * CH]
     start_core(1)
+    pack_rims(own.at[1], 2)
+    pack_rims(own.at[2], 3)
+    halo_h = halo_copies(2, tab_h)
+    halo_p = halo_copies(3, tab_p)
+    for copy in halo_h + halo_p:
+        copy.start()
     pre_grad_t = own[2].reshape(BLK * VOX, CH).astype(F32).T.astype(BF16)
     for kx in range(3):
         part = dot(pre_grad_t, columns(y_m, kx))

time: 89.2 us -> 89.7 us (level)
  no operation moved by 1% of the time
where the time goes in v10:
time: 89.7 us; the launch traced here: 89.3 us
  Pallas kernels  88.5 us (99%)
    pallas_call x1, Pallas kernels, per_device(): pl.pallas_call(functools.partial(unit_kernel, n_tile, n_dev, scale), out_...  84.7 us
    pallas_call x1, Pallas kernels, per_device(): pl.pallas_call(finish_kernel, out_shape=(jax.ShapeDtypeStruct(features.sh...  3.77 us

profile of v10, /device:TPU:1, one launch (start us, length us, event | category | flops | bytes accessed | tf_op | source)
XLA Modules:
  0.0 89.3 jit_solution(13481851235690323243)
XLA Ops:
  0.6 84.7 %shard_map.111 = (bf16[8,64,128]{2,1,0:T(8,128)(2,1)}, bf16[8,64,128]{2,1,0:T(8,128)(2,1)}, bf16[2,2,4,4,8,16,128]{6,5,4,3,2,1,0:T(8,128)(2,1)}) custom-call(s32[8]{0:T(128)} %pos_in.1, s32[8,27]{1,0:T(8,128)} %nbr_in.1, s32[4]{0:T(128)} %rim_in.1, bf16[8,64,128]{2,1,0:T(8,128)(2,1)} %feat_in.1, bf16[8,64,128]{2,1,0:T(8,128)(2,1)} %cot_in.1, ...), custom_call_target="tpu_custom_call" | custom-call | tf_op jit(solution)/shard_map/pallas_call | solution.py:636
  85.4 3.8 %shard_map.112 = (bf16[8,64,128]{2,1,0:T(8,128)(2,1)}, bf16[8,64,128]{2,1,0:T(8,128)(2,1)}, f32[3456,128]{1,0:T(8,128)}, f32[3456,128]{1,0:T(8,128)}) custom-call(bf16[2,2,4,4,8,16,128]{6,5,4,3,2,1,0:T(8,128)(2,1)} %get-tuple-element.7.sums, bf16[8,64,128]{2,1,0:T(8,128)(2,1)} %get-tuple-element.8.output_in, bf16[8,64,128]{2,1,0:T(8,128)(2,1)} %get-tuple-element.9.grad_in), custom_call_target="tpu_custom_call" | custom-call | tf_op jit(solution)/shard_map/pallas_call | solution.py:725
